TPU v7x, 128 devices: a whole 4x4x4 slice. The times are simulated.
128 devices in a mesh: member: 4 (over z), region: 32 (over y, x, core).
Axes of the slice: x: 4, y: 4, z: 4, core: 2. Of those that a mesh axis runs over, the one named last changes fastest.
Arguments:
- grid_input: bfloat16 [16, 16384, 1024], P('member', 'region'), may hold values from -6 to 6
- w_hidden: bfloat16 [1024, 1024], replicated, may hold values from -0.1875 to 0.1875
- b_hidden: float32 [1024], replicated, may hold values from -3 to 3
- w_out: bfloat16 [1024, 96], replicated, may hold values from -0.1875 to 0.1875
- b_out: float32 [96], replicated, may hold values from -3 to 3
- target: float32 [96, 16384], P(None, 'region'), may hold values from -6 to 6
- channel_weight: float32 [96], replicated, may hold values from 0.5 to 5
- interp_weight: bfloat16 [128, 3, 128, 128], P('region'), may hold values from -0.5 to 0.5
- block_index: int32 [128, 3], P('region'), may hold values from 0 to 63, as said below
Outputs:
- grad_w_hidden: float32 [1024, 1024], P(('member', 'region'))
- grad_w_out: float32 [1024, 96], P(('member', 'region'))
- grad_mesh: float32 [16, 8192, 1024], P('member', 'region')
Inputs may be any that keep to these rules, and one draw needn't show every extreme that they name: `block_index`: grid block b lies in region b // 4; its mesh blocks belong to that region or to one of its two neighbours along the region index, cyclically, a block j belonging to region j // 2. For k = 0 the mesh block is the region's own block number (b % 4) % 2.
All inputs are finite; a program needn't handle non-finite values.
Results may differ from a plain program's by a relative error of at most 0.0095.
Values may be sent and summed in bfloat16 or wider, within the bound.
A program may use at most 128 MiB of HBM per device.

v0:
```python
import jax
import jax.numpy as jnp
from jax import lax
from jax.sharding import PartitionSpec as P

GB = 128
MB = 128
K = 3
GBLK_REG = 4
MBLK_REG = 2


ALPHA = 0.95
SMOOTH = 0.25


def shifted(block, axis, distance):
    devices = range(lax.axis_size(axis))
    route = [((i - distance) % len(devices), i) for i in devices]
    return lax.ppermute(block, axis, route)


def smooth_slope(diff):
    return diff / jnp.sqrt(diff * diff + SMOOTH * SMOOTH)


def ensemble_adjoint(own, every, target_cells, channel_weight):
    members = every.shape[0]
    kappa = ALPHA / (2.0 * members * (members - 1)) + (1.0 - ALPHA) / (2.0 * members * members)
    skill = smooth_slope(own - target_cells[None]) / members
    spread = jnp.sum(smooth_slope(own[:, None] - every[None, :]), axis=1)
    return channel_weight[None, :, None] * (skill - 2.0 * kappa * spread)


def body(
    grid_input, w_hidden, b_hidden, w_out, b_out, target, channel_weight, interp_weight, block_index
):
    members_here = grid_input.shape[0]
    cells_here = grid_input.shape[1]
    width = grid_input.shape[2]
    channels = w_out.shape[1]
    flat_input = grid_input.reshape(members_here * cells_here, width)
    pre_act = jnp.dot(flat_input, w_hidden, preferred_element_type=jnp.float32) + b_hidden
    activated = jax.nn.silu(pre_act).astype(jnp.bfloat16)
    predicted = jnp.dot(activated, w_out, preferred_element_type=jnp.float32) + b_out
    pred_cols = predicted.reshape(members_here, cells_here, channels).transpose(0, 2, 1)
    cell_slices = lax.all_to_all(pred_cols, "member", split_axis=2, concat_axis=0, tiled=True)
    slice_len = cell_slices.shape[2]
    slice_start = lax.axis_index("member") * slice_len
    target_slice = lax.dynamic_slice_in_dim(target, slice_start, slice_len, 1)
    adjoint = ensemble_adjoint(cell_slices, cell_slices, target_slice, channel_weight).astype(
        jnp.bfloat16
    )
    adjoint_cols = lax.all_to_all(adjoint, "member", split_axis=0, concat_axis=2, tiled=True)
    dpred = adjoint_cols.transpose(0, 2, 1).reshape(members_here * cells_here, channels)
    dact = jnp.dot(dpred, w_out.T, preferred_element_type=jnp.float32)
    logistic = jax.nn.sigmoid(pre_act)
    dpre = (dact * logistic * (1.0 + pre_act * (1.0 - logistic))).astype(jnp.bfloat16)
    hidden_term = lax.dot_general(
        flat_input, dpre, (((0,), (0,)), ((), ())), preferred_element_type=jnp.float32
    )
    output_term = lax.dot_general(
        activated, dpred, (((0,), (0,)), ((), ())), preferred_element_type=jnp.float32
    )
    summed = lax.psum_scatter(
        jnp.concatenate([hidden_term, output_term], axis=1),
        ("member", "region"),
        scatter_dimension=0,
        tiled=True,
    )
    grad_w_hidden = summed[:, :width]
    grad_w_out = summed[:, width:]
    dinput = jnp.dot(dpre, w_hidden.T, preferred_element_type=jnp.float32).astype(jnp.bfloat16)
    dinput_blocks = dinput.reshape(members_here, GBLK_REG, GB, width)
    region_now = lax.axis_index("region")
    region_count = lax.axis_size("region")
    owner = block_index // MBLK_REG
    relative = (owner - region_now + 1 + region_count) % region_count
    target_slots = (relative * MBLK_REG + block_index % MBLK_REG).reshape(-1)
    buffer = jnp.zeros((members_here, 3 * MBLK_REG, MB, width), jnp.float32)

    def add_block(pair_pos, accum):
        block_pos = pair_pos // K
        source_pos = pair_pos % K
        weight_tile = lax.dynamic_index_in_dim(
            lax.dynamic_index_in_dim(interp_weight, block_pos, 0, False), source_pos, 0, False
        )
        block_rows = lax.dynamic_index_in_dim(dinput_blocks, block_pos, 1, False)
        contrib = jnp.einsum(
            "gn,mgh->mnh", weight_tile, block_rows, preferred_element_type=jnp.float32
        )
        target_slot = lax.dynamic_index_in_dim(target_slots, pair_pos, 0, False)
        current = lax.dynamic_index_in_dim(accum, target_slot, 1, False)
        return lax.dynamic_update_index_in_dim(accum, current + contrib, target_slot, 1)

    buffer = lax.fori_loop(0, GBLK_REG * K, add_block, buffer)
    from_above = shifted(buffer[:, :MBLK_REG], "region", -1)
    from_below = shifted(buffer[:, 2 * MBLK_REG :].astype(jnp.bfloat16), "region", 1).astype(
        jnp.float32
    )
    own_terms = buffer[:, MBLK_REG : 2 * MBLK_REG] + from_above + from_below
    grad_mesh = own_terms.reshape(members_here, MBLK_REG * MB, width)
    return (grad_w_hidden, grad_w_out, grad_mesh)


def solution(mesh):
    placed = (
        P("member", "region", None),
        P(),
        P(),
        P(),
        P(),
        P(None, "region"),
        P(),
        P("region", None, None, None),
        P("region", None),
    )
    return jax.shard_map(
        body,
        mesh=mesh,
        in_specs=placed,
        out_specs=(
            P(("member", "region"), None),
            P(("member", "region"), None),
            P("member", "region", None),
        ),
        check_vma=False,
    )
```

profile of v0, /device:TPU:0, one launch (start us, length us, event | category | flops | bytes accessed | tf_op | source)
XLA Modules:
  0.0 376.6 jit_solution(13426458161038298176)
XLA Ops:
  7.2 1.6 copy-done
  8.8 10.3 %multiply_convert_fusion.1 = (bf16[2048,1024]{1,0:T(8,128)(2,1)S(1)}, f32[2048,1024]{1,0:T(8,128)}) fusion(f32[1024]{0:T(1024)} %param.13, bf16[2048,1024]{1,0:T(8,128)(2,1)} %bitcast.75, bf16[1024,1024]{1,0:T(8,128)(2,1)S(1)} %copy-done), kind=kOutput, calls=%fused_computation.14 | convolution fusion | flops 4307550208 | bytes 18878464 | tf_op jit(solution)/shard_map/dot_general | solution.py:43
  19.0 2.0 copy-done.2
  21.0 1.4 convolution_add_fusion
  22.5 1.4 reshape.35
  23.9 2.3 copy.39
  26.1 5.4 %all-to-all-start = ((f32[4,96,512]{1,0,2:T(4,128)}), f32[4,96,512]{1,0,2:T(4,128)S(1)}, u32[]{:S(2)}, u32[]{:S(2)}) async-start(f32[4,96,512]{1,0,2:T(4,128)} %bitcast.67), calls=%async_computation | async-start | bytes 2097152 | tf_op jit(solution)/shard_map/all_to_all | solution.py:47
  31.5 0.8 constant_dynamic-slice_fusion.2
  32.4 14.3 %all-to-all-done = f32[4,96,512]{1,0,2:T(4,128)S(1)} async-done(((f32[4,96,512]{1,0,2:T(4,128)}), f32[4,96,512]{1,0,2:T(4,128)S(1)}, u32[]{:S(2)}, u32[]{:S(2)}) %all-to-all-start) | async-done | bytes 786464 | tf_op jit(solution)/shard_map/all_to_all | solution.py:47
  46.6 1.3 copy.41
  48.0 4.0 %fusion.7 = f32[16,96,128]{2,1,0:T(8,128)S(1)} fusion(f32[16,96,128]{2,1,0:T(8,128)} %bitcast.69), kind=kLoop, calls=%fused_computation.12 | loop fusion | flops 15532032 | bytes 1572864 | tf_op jit(solution)/shard_map/reduce_sum | solution.py:31
  52.0 1.1 multiply_convert_fusion.2
  53.1 3.5 all-to-all-start.1
  56.9 7.0 %all-to-all-done.1 = bf16[16,96,128]{2,1,0:T(8,128)(2,1)S(1)} async-done(((bf16[16,96,128]{2,1,0:T(8,128)(2,1)}), bf16[16,96,128]{2,1,0:T(8,128)(2,1)S(1)}, u32[]{:S(2)}, u32[]{:S(2)}) %all-to-all-start.1) | async-done | bytes 393248 | tf_op jit(solution)/shard_map/all_to_all | solution.py:54
  64.4 5.8 %multiply_convert_fusion = bf16[2048,1024]{1,0:T(8,128)(2,1)S(1)} fusion(f32[2048,1024]{1,0:T(8,128)} %get-tuple-element.215, bf16[2048,96]{0,1:T(8,128)(2,1)S(1)} %bitcast.70, bf16[1024,96]{0,1:T(8,128)(2,1)S(1)} %copy-done.5, f32[1024]{0:T(1024)S(1)} %copy-done.10), kind=kOutput, calls=%fused_computation.13 | convolution fusion | flops 423624704 | bytes 13176832 | tf_op jit(solution)/shard_map/dot_general | solution.py:56
  70.2 6.3 %convolution_convert_fusion = bf16[2048,1024]{1,0:T(8,128)(2,1)} fusion(bf16[2048,1024]{1,0:T(8,128)(2,1)S(1)} %multiply_convert_fusion, bf16[1024,1024]{1,0:T(8,128)(2,1)S(1)} %copy-done), kind=kOutput, calls=%fused_computation.19 | convolution fusion | flops 4297064448 | bytes 10485760 | tf_op jit(solution)/shard_map/dot_general | solution.py:73
  76.5 5.9 %broadcast_in_dim.21 = f32[4,6,128,1024]{2,3,0,1:T(8,128)} broadcast(f32[]{:T(128)} %constant.225.clone.1), dimensions={} | broadcast | bytes 12582916 | tf_op jit(solution)/shard_map/broadcast_in_dim | solution.py:80
  82.5 88.7 %while.16 = (s32[]{:T(128)}, f32[4,6,128,1024]{2,3,0,1:T(8,128)}, s32[12]{0:T(128)S(1)}, bf16[4,4,128,1024]{3,2,1,0:T(8,128)(2,1)}, bf16[4,3,128,128]{3,2,1,0:T(...) while((s32[]{:T(128)}, f32[4,6,128,1024]{2,3,0,1:T(8,128)}, ...), condition=%wide.region_3.4_spmd, body=%wide.region_2.3_spmd.sunk | while | flops 134742048 | bytes 9470358 | solution.py:96
  82.5 0.6 dynamic_slice.67
  85.0 1.7 constant_dynamic-slice_fusion.4
  86.8 3.1 bitcast_dynamic-update-slice_fusion.2
  89.9 0.6 dynamic_slice.67
  92.4 1.7 constant_dynamic-slice_fusion.4
  94.2 3.1 bitcast_dynamic-update-slice_fusion.2
  97.3 0.6 dynamic_slice.67
  99.8 1.7 constant_dynamic-slice_fusion.4
  101.6 3.0 bitcast_dynamic-update-slice_fusion.2
  104.7 0.6 dynamic_slice.67
  107.2 1.7 constant_dynamic-slice_fusion.4
  109.0 3.1 bitcast_dynamic-update-slice_fusion.2
  112.1 0.6 dynamic_slice.67
  114.6 1.7 constant_dynamic-slice_fusion.4
  116.4 3.1 bitcast_dynamic-update-slice_fusion.2
  119.5 0.6 dynamic_slice.67
  122.0 1.7 constant_dynamic-slice_fusion.4
  123.8 3.0 bitcast_dynamic-update-slice_fusion.2
  126.8 0.6 dynamic_slice.67
  129.4 1.7 constant_dynamic-slice_fusion.4
  131.1 3.1 bitcast_dynamic-update-slice_fusion.2
  134.2 0.6 dynamic_slice.67
  136.7 1.7 constant_dynamic-slice_fusion.4
  138.5 3.1 bitcast_dynamic-update-slice_fusion.2
  141.6 0.6 dynamic_slice.67
  144.1 1.7 constant_dynamic-slice_fusion.4
  145.9 3.0 bitcast_dynamic-update-slice_fusion.2
  151.5 1.7 constant_dynamic-slice_fusion.4
  153.3 3.1 bitcast_dynamic-update-slice_fusion.2
  158.9 1.7 constant_dynamic-slice_fusion.4
  160.7 3.1 bitcast_dynamic-update-slice_fusion.2
  166.3 1.7 constant_dynamic-slice_fusion.4
  168.1 3.1 bitcast_dynamic-update-slice_fusion.2
  171.2 4.8 %slice.19 = f32[4,2,128,1024]{2,3,0,1:T(8,128)} slice(f32[4,6,128,1024]{2,3,0,1:T(8,128)} %get-tuple-element.163), slice={[0:4], [0:2], [0:128], [0:1024]} | slice | bytes 8388608 | tf_op jit(solution)/shard_map/slice | solution.py:97
  176.0 2.3 collective-permute-start
  178.3 0.8 fusion.14
  179.1 4.8 %convolution_bitcast_fusion = f32[1024,1024]{0,1:T(8,128)S(1)} fusion(bf16[2048,1024]{1,0:T(8,128)(2,1)S(1)} %copy-done.12, bf16[2048,1024]{1,0:T(8,128)(2,1)S(1)} %bitcast.76), kind=kOutput, calls=%fused_computation.21 | convolution fusion | flops 4294967296 | bytes 12582912 | tf_op jit(solution)/shard_map/dot_general | solution.py:59
  183.9 2.6 pad_maximum_fusion
  186.5 2.5 slice.24
  189.2 165.0 %all-reduce.3.cloned.1.call-done = f32[1024,1120]{0,1:T(8,128)} async-done(((f32[1024,1120]{0,1:T(8,128)}), f32[1024,1120]{0,1:T(8,128)}) %all-reduce.3.cloned.1.call-update) | async-done | bytes 4587536
  354.2 1.2 constant_dynamic-slice_fusion.1
  355.4 0.8 copy.46
  356.2 0.9 dynamic-slice.10
  357.1 0.7 copy.47
  357.8 6.6 %convert_add_fusion = f32[4,2,128,1024]{2,3,0,1:T(8,128)} fusion(bf16[4,2,128,1024]{2,3,0,1:T(8,128)(2,1)} %collective-permute-done.1, f32[4,2,128,1024]{2,3,0,1:T(8,128)} %collective-permute-done, f32[4,6,128,1024]{2,3,0,1:T(8,128)} %get-tuple-element.163), kind=kLoop, calls=%fused_computation.18 | loop fusion | flops 3145728 | bytes 14680064 | tf_op jit(solution)/shard_map/add | solution.py:101
  364.4 5.3 %copy.45 = f32[4,2,128,1024]{3,2,1,0:T(8,128)} copy(f32[4,2,128,1024]{2,3,0,1:T(8,128)} %convert_add_fusion) | data formatting | bytes 8388608 | tf_op jit(solution)/shard_map/add | solution.py:101
  (37 shorter events, 2.7 us)
Async XLA Ops:
  7.2 1.6 copy-start
  8.8 12.3 %copy-start.5 = (bf16[1024,96]{0,1:T(8,128)(2,1)S(1)}, bf16[1024,96]{0,1:T(8,128)(2,1)}, u32[]{:S(2)}) copy-start(bf16[1024,96]{0,1:T(8,128)(2,1)} %param.14) | copy-start | bytes 589828
  8.8 12.3 %copy-start.7 = (f32[96]{0:T(128)S(1)}, f32[96]{0:T(128)}, u32[]{:S(2)}) copy-start(f32[96]{0:T(128)} %param.15) | copy-start | bytes 1156
  19.0 2.0 copy-start.2
  26.1 20.5 %all-to-all-start = ((f32[4,96,512]{1,0,2:T(4,128)}), f32[4,96,512]{1,0,2:T(4,128)S(1)}, u32[]{:S(2)}, u32[]{:S(2)}) async-start(f32[4,96,512]{1,0,2:T(4,128)} %bitcast.67), calls=%async_computation | async-start | bytes 2097152 | tf_op jit(solution)/shard_map/all_to_all | solution.py:47
  31.5 20.4 %copy-start.8 = (f32[96]{0:T(128)S(1)}, f32[96]{0:T(128)}, u32[]{:S(2)}) copy-start(f32[96]{0:T(128)} %param.17) | copy-start | bytes 1156
  47.9 4.0 %copy-start.4 = (f32[4,4,96,128]{3,2,1,0:T(8,128)S(1)}, f32[4,4,96,128]{3,2,1,0:T(8,128)}, u32[]{:S(2)}) copy-start(f32[4,4,96,128]{3,2,1,0:T(8,128)} %copy.41) | copy-start | bytes 2359300
  47.9 8.8 %copy-start.6 = (s32[4,3]{1,0:T(4,128)S(1)}, s32[4,3]{1,0:T(4,128)}, u32[]{:S(2)}) copy-start(s32[4,3]{1,0:T(4,128)} %param.19) | copy-start | bytes 148
  48.0 16.4 %copy-start.10 = (f32[1024]{0:T(1024)S(1)}, f32[1024]{0:T(1024)}, u32[]{:S(2)}) copy-start(f32[1024]{0:T(1024)} %param.13) | copy-start | bytes 12292
  53.1 10.8 %all-to-all-start.1 = ((bf16[16,96,128]{2,1,0:T(8,128)(2,1)}), bf16[16,96,128]{2,1,0:T(8,128)(2,1)S(1)}, u32[]{:S(2)}, u32[]{:S(2)}) async-start(bf16[16,96,128]{2,1,0:T(8,128)(2,1)} %multiply_convert_fusion.2), calls=%async_computation.1 | async-start | bytes 786432 | tf_op jit(solution)/shard_map/all_to_all | solution.py:54
  56.5 297.7 %all-reduce.3.cloned.1.call-start = ((), (), s32[]{:S(2)}) async-start(), calls=%async_computation.2 | async-start | bytes 9175040
  70.2 6.3 %copy-start.11 = (bf16[2048,1024]{1,0:T(8,128)(2,1)}, bf16[2048,1024]{1,0:T(8,128)(2,1)S(1)}, u32[]{:S(2)}) copy-start(bf16[2048,1024]{1,0:T(8,128)(2,1)S(1)} %multiply_convert_fusion) | copy-start | bytes 12582916
  171.2 7.1 %copy-start.3 = (bf16[2048,1024]{1,0:T(8,128)(2,1)S(1)}, bf16[2048,1024]{1,0:T(8,128)(2,1)}, u32[]{:S(2)}) copy-start(bf16[2048,1024]{1,0:T(8,128)(2,1)} %copy-done.2) | copy-start | bytes 12582916
  171.2 7.9 %copy-start.12 = (bf16[2048,1024]{1,0:T(8,128)(2,1)S(1)}, bf16[2048,1024]{1,0:T(8,128)(2,1)}, u32[]{:S(2)}) copy-start(bf16[2048,1024]{1,0:T(8,128)(2,1)} %copy-done.11) | copy-start | bytes 12582916
  176.0 3.1 copy-start.9
  176.0 181.8 %collective-permute-start = (f32[4,2,128,1024]{2,3,0,1:T(8,128)}, f32[4,2,128,1024]{2,3,0,1:T(8,128)}, u32[]{:S(2)}, u32[]{:S(2)}) collective-permute-start(f32[4,2,128,1024]{2,3,0,1:T(8,128)} %slice.19), channel_id=1, source_target_pairs={{1,0},{2,1},{3,2},{4,3},{5,4},{6,5},{7,6},{8,7},{9,8},{10,9},{11,1... | collective-permute-start | bytes 12582920 | tf_op jit(solution)/shard_map/ppermute | solution.py:20
  189.1 168.7 %collective-permute-start.1 = (bf16[4,2,128,1024]{2,3,0,1:T(8,128)(2,1)S(1)}, bf16[4,2,128,1024]{2,3,0,1:T(8,128)(2,1)}, u32[]{:S(2)}, u32[]{:S(2)}) collective-permute-start(bf16[4,2,128,1024]{2,3,0,1:T(8,128)(2,1)S(1)} %slice.24), channel_id=1, source_target_pairs={{31,0},{0,1},{1,2},{2,3},{3,4},{4,5},{5,6},{6,7},{7,8},{8,9},{9,10... | collective-permute-start | bytes 6291464 | tf_op jit(solution)/shard_map/ppermute | solution.py:20
  357.8 12.0 %copy-start.1 = (bf16[1024,1024]{1,0:T(8,128)(2,1)S(1)}, bf16[1024,1024]{1,0:T(8,128)(2,1)}, u32[]{:S(2)}) copy-start(bf16[1024,1024]{1,0:T(8,128)(2,1)} %param.12) | copy-start | bytes 6291460
Sparse Core Ops, SparseCore 0:
  186.7 167.4 all-reduce.2
where the time goes:
time: 379 us; the launch traced here: 377 us
  waiting for transfers between devices  186 us (49%)
  matrix products  66.4 us (18%)
  local copies, waits for them, and re-layouts  59.9 us (16%)
  loops' own time  23.9 us (6%)
  other arithmetic  14.4 us (4%)
  between operations  14.2 us (4%)
  starting transfers between devices  11.5 us (3%)
    unnamed x2, waiting for transfers between devices  165 us
    dot_general x12, matrix products, add_block(): jnp.einsum('gn,mgh->mnh', weight_tile, block_rows, preferred_element_type...  37 us
    another operation x1, loops' own time, body(): buffer = lax.fori_loop(0, GBLK_REG * K, add_block, buffer)  23.9 us
    dynamic_slice x12, local copies, waits for them, and re-layouts, add_block(): current = lax.dynamic_index_in_dim(accum, target_slot, 1, False)  20.8 us
    all_to_all x1, waiting for transfers between devices, body(): lax.all_to_all(pred_cols, 'member', split_axis=2, concat_axis=0, tiled=True)  14.3 us
    dot_general x1, matrix products, body(): jnp.dot(flat_input, w_hidden, preferred_element_type=jnp.float32) + b_hidden  10.3 us
  transfers between devices with their start and end apart: 5, of which 3 were waited for; matrix products, arithmetic and copies ran while one was open for 4% of the time, Pallas kernels for 0%

commit v1 on v0

v1 whole, which is shorter than its diff:
```python
import jax
import jax.numpy as jnp
from jax import lax
from jax.experimental import pallas as pl
from jax.experimental.pallas import tpu as pltpu
from jax.sharding import PartitionSpec as P

MESH = pl.DeviceIdType.MESH
F32 = jnp.float32
BF16 = jnp.bfloat16
M = 16
ALPHA = 0.95
SMOOTH = 0.25
KAPPA = ALPHA / (2.0 * M * (M - 1)) + (1.0 - ALPHA) / (2.0 * M * M)
CA = 640
CW = 1152


def kernel(
    x_hbm, wh_hbm, wot_hbm, bh_ref, bo_ref, cw_ref, tgt_hbm, tile_hbm, bi_ref,
    gh_ref, go_ref, mesh_hbm,
    xv, wh, wot, tiles, tgt, act, dsil, dpre, wt, bcol, ccol,
    predsend, predrecv, pf, adjf, adjsend, adjrecv, outt,
    own, send_dn, send_up, recv_dn, recv_up,
    accf, csend, crecv, s1a, s1b, r1a, r1b, p2a, p2b, s2a, s2b, r2a, r2b, p3, r3,
    load_sem, x_sem, pred_ss, pred_rs, adj_ss, adj_rs, dn_ss, dn_rs, up_ss, up_rs,
    c_ss, c_rs, a1_ss, a1_rs, b1_ss, b1_rs, a2_ss, a2_rs, b2_ss, b2_rs, x_ss, x_rs, out_sem,
):
    z = lax.axis_index("member")
    r = lax.axis_index("region")
    yy, xx, cc = r // 8, (r // 2) % 4, r % 2
    oc = 1 - cc

    def zdev(k):
        return ((z + k) % 4, r)

    def ydev(k):
        return (z, ((yy + k) % 4) * 8 + xx * 2 + cc)

    def xdev(k):
        return (z, yy * 8 + ((xx + k) % 4) * 2 + cc)

    partner = (z, r + 1 - 2 * cc)
    up = (z, (r + 1) % 32)
    down = (z, (r + 31) % 32)

    def block_of(i):
        return (z + 1 + i) % 4

    load_wh = pltpu.make_async_copy(wh_hbm, wh, load_sem.at[0])
    load_wh.start()

    def x_copy(i):
        start = pl.multiple_of(block_of(i) * 128, 128)
        return pltpu.make_async_copy(
            x_hbm.at[:, pl.ds(start, 128), :], xv.at[i], x_sem.at[i]
        )

    x_copy(0).start()
    load_wot = pltpu.make_async_copy(wot_hbm, wot, load_sem.at[1])
    load_wot.start()
    for i in range(1, 4):
        x_copy(i).start()
    load_tiles = pltpu.make_async_copy(tile_hbm, tiles, load_sem.at[2])
    load_tiles.start()
    load_tgt = pltpu.make_async_copy(
        tgt_hbm.at[:, pl.ds(pl.multiple_of(z * 128, 128), 128)], tgt, load_sem.at[3]
    )
    load_tgt.start()

    barrier = pltpu.get_barrier_semaphore()
    peers = [f(k) for f in (zdev, ydev, xdev) for k in (1, 2, 3)] + [up, down]
    for peer in peers:
        pl.semaphore_signal(barrier, inc=1, device_id=peer, device_id_type=MESH)
    pl.semaphore_wait(barrier, len(peers))

    def pred_copy(i):
        return pltpu.make_async_remote_copy(
            src_ref=predsend.at[i], dst_ref=predrecv.at[i],
            send_sem=pred_ss.at[i], recv_sem=pred_rs.at[i],
            device_id=zdev(i + 1), device_id_type=MESH,
        )

    load_wh.wait()
    load_wot.wait()

    def forward(i, carry):
        x_copy(i).wait()
        xb = xv[i].reshape(512, 1024)
        for n in range(4):
            cols = slice(n * 256, n * 256 + 256)
            pre = jnp.dot(xb, wh[:, cols], preferred_element_type=F32) + bh_ref[:, cols]
            sig = 0.5 + 0.5 * jnp.tanh(0.5 * pre)
            silu = pre * sig
            act[i, :, :, cols] = silu.astype(BF16).reshape(4, 128, 256)
            dsil[i, :, :, cols] = (sig + silu * (1.0 - sig)).reshape(4, 128, 256)
        predt = lax.dot_general(
            wot[...], act[i].reshape(512, 1024), (((1,), (1,)), ((), ())),
            preferred_element_type=F32,
        ).astype(BF16)
        for m in range(4):
            predsend[i, m] = predt[:, m * 128 : m * 128 + 128]

        @pl.when(i < 3)
        def _():
            pred_copy(i).start()

        return carry

    lax.fori_loop(0, 4, forward, 0)

    load_tiles.wait()

    def build(i, carry):
        b = block_of(i)
        slots = []
        turned = []
        for k in range(3):
            index = bi_ref[b, k]
            relative = (index // 2 - r + 33) % 32
            slots.append(relative * 2 + index % 2)
            turned.append(tiles[b, k].astype(F32).T)
        for s in range(6):
            total = None
            for k in range(3):
                term = turned[k] * jnp.where(slots[k] == s, 1.0, 0.0)
                total = term if total is None else total + term
            wt[i, s * 128 : s * 128 + 128, :] = total.astype(BF16)
        return carry

    lax.fori_loop(0, 4, build, 0)

    bcol[...] = jnp.zeros_like(bcol)
    ccol[...] = jnp.zeros_like(ccol)
    bcol[:, :96] = jnp.broadcast_to(bo_ref[...], (128, 96))
    ccol[:, :96] = jnp.broadcast_to(cw_ref[...], (128, 96))
    bcol[...] = bcol[...].T
    ccol[...] = ccol[...].T
    load_tgt.wait()

    pf[12:16] = predsend[3].astype(F32)
    for i in range(3):
        pred_copy(i).wait_recv()
        pf[4 * i : 4 * i + 4] = predrecv[i].astype(F32)

    def score(t, carry):
        rows = pl.ds(pl.multiple_of(t * 8, 8), 8)
        p = pf[:, rows, :]
        aim = tgt[rows, :] - bcol[rows, :]

        def slope(d):
            return d * lax.rsqrt(d * d + SMOOTH * SMOOTH)

        spread = None
        for k in range(1, 8):
            s = slope(p - jnp.concatenate([p[k:], p[:k]], axis=0))
            change = s - jnp.concatenate([s[16 - k :], s[: 16 - k]], axis=0)
            spread = change if spread is None else spread + change
        s = slope(p[:8] - p[8:])
        spread = spread + jnp.concatenate([s, -s], axis=0)
        skill = slope(p - aim[None])
        adjf[:, rows, :] = ccol[rows, :][None] * (skill * (1.0 / M) - 2.0 * KAPPA * spread)
        return carry

    lax.fori_loop(0, 12, score, 0)

    def adj_copy(m, i):
        return pltpu.make_async_remote_copy(
            src_ref=adjsend.at[m, i], dst_ref=adjrecv.at[m, i],
            send_sem=adj_ss.at[m, i], recv_sem=adj_rs.at[m, i],
            device_id=zdev(3 - i), device_id_type=MESH,
        )

    for m in range(4):
        for i in range(3):
            adjsend[m, i] = adjf[4 * i + m].astype(BF16)
            adj_copy(m, i).start()
        adjrecv[m, 3] = adjf[12 + m].astype(BF16)

    def dn_copy(m):
        return pltpu.make_async_remote_copy(
            src_ref=send_dn.at[m], dst_ref=recv_dn.at[m],
            send_sem=dn_ss.at[m], recv_sem=dn_rs.at[m],
            device_id=down, device_id_type=MESH,
        )

    def up_copy(m):
        return pltpu.make_async_remote_copy(
            src_ref=send_up.at[m], dst_ref=recv_up.at[m],
            send_sem=up_ss.at[m], recv_sem=up_rs.at[m],
            device_id=up, device_id_type=MESH,
        )

    outt[...] = jnp.zeros_like(outt)

    def backward(m, carry):
        for i in range(3):
            adj_copy(m, i).wait_recv()
        adj = jnp.concatenate([adjrecv[m, i] for i in range(4)], axis=1)
        for n in range(4):
            cols = slice(n * 256, n * 256 + 256)
            dact = lax.dot_general(
                adj, wot[:, cols], (((0,), (0,)), ((), ())), preferred_element_type=F32
            )
            grad = dact * dsil[:, m, :, cols].reshape(512, 256)
            dpre[:, m, :, cols] = grad.astype(BF16).reshape(4, 128, 256)
        outt[:96, :] += jnp.dot(
            adj, act[:, m].reshape(512, 1024), preferred_element_type=F32
        )
        dp = dpre[:, m].reshape(512, 1024)
        lhs = jnp.concatenate([wt[i] for i in range(4)], axis=1)
        for n in range(4):
            cols = slice(n * 256, n * 256 + 256)
            dinput = lax.dot_general(
                dp, wh[cols, :], (((1,), (1,)), ((), ())), preferred_element_type=F32
            ).astype(BF16)
            contrib = jnp.dot(lhs, dinput, preferred_element_type=F32)
            send_dn[m, :, cols] = contrib[:256].astype(BF16)
            own[m, :, cols] = contrib[256:512]
            send_up[m, :, cols] = contrib[512:].astype(BF16)
        dn_copy(m).start()
        up_copy(m).start()
        return carry

    lax.fori_loop(0, 4, backward, 0)

    turned_out = outt[...].T.reshape(4, 4, 4, 2, 8, 128)
    for c in range(2):
        accf[c, :, :, :, 1024:] = turned_out[:, :, :, c].reshape(4, 4, 32, 128)

    def c_copy(zc):
        return pltpu.make_async_remote_copy(
            src_ref=csend.at[zc], dst_ref=crecv.at[zc],
            send_sem=c_ss.at[zc], recv_sem=c_rs.at[zc],
            device_id=partner, device_id_type=MESH,
        )

    def weights(zc, carry):
        start = pl.multiple_of(zc * 256, 256)
        lhs = xv[:, :, :, pl.ds(start, 256)].reshape(2048, 256)
        for n in range(2):
            cols = slice(n * 512, n * 512 + 512)
            part = lax.dot_general(
                lhs, dpre[:, :, :, cols].reshape(2048, 512), (((0,), (0,)), ((), ())),
                preferred_element_type=F32,
            ).reshape(4, 4, 2, 8, 512)
            for c in range(2):
                accf[c, zc, :, :, cols] = part[:, :, c].reshape(4, 32, 512)
        csend[zc] = accf[oc, zc].astype(BF16)
        c_copy(zc).start()
        return carry

    lax.fori_loop(0, 4, weights, 0)

    def combine(zc, carry):
        c_copy(zc).wait_recv()
        total = accf[cc, zc] + crecv[zc].astype(F32)
        accf[cc, zc] = total
        s1a[zc] = total[:, :, :CA].astype(BF16)
        s1b[:, zc] = total[:, :, CA:].astype(BF16)
        return carry

    lax.fori_loop(0, 4, combine, 0)

    def remote(src, dst, ss, rs, dev, k):
        return pltpu.make_async_remote_copy(
            src_ref=src, dst_ref=dst, send_sem=ss.at[k - 1], recv_sem=rs.at[k - 1],
            device_id=dev, device_id_type=MESH,
        )

    def a1(k):
        return remote(s1a.at[(z + k) % 4], r1a.at[k - 1], a1_ss, a1_rs, zdev(k), k)

    def b1(k):
        return remote(s1b.at[(yy + k) % 4], r1b.at[k - 1], b1_ss, b1_rs, ydev(k), k)

    def a2(k):
        return remote(s2a.at[(yy + k) % 4], r2a.at[k - 1], a2_ss, a2_rs, ydev(k), k)

    def b2(k):
        return remote(s2b.at[(z + k) % 4], r2b.at[k - 1], b2_ss, b2_rs, zdev(k), k)

    def x3(k):
        return remote(p3.at[(xx + k) % 4], r3.at[k - 1], x_ss, x_rs, xdev(k), k)

    for k in (2, 1, 3):
        a1(k).start()
        b1(k).start()

    def out_copy(m):
        return pltpu.make_async_copy(own.at[m], mesh_hbm.at[m], out_sem.at[m])

    def finish(m, carry):
        dn_copy(m).wait_recv()
        up_copy(m).wait_recv()
        own[m] = own[m] + recv_dn[m].astype(F32) + recv_up[m].astype(F32)
        out_copy(m).start()
        return carry

    lax.fori_loop(0, 2, finish, 0)

    for k in (1, 3, 2):
        a1(k).wait_recv()
    total = accf[cc, z, :, :, :CA]
    for k in range(3):
        total = total + r1a[k].astype(F32)
    p2a[...] = total
    s2a[...] = total.astype(BF16)
    for k in (2, 1, 3):
        a2(k).start()
    for k in (1, 3, 2):
        b1(k).wait_recv()
    total = accf[cc, :, yy, :, CA:]
    for k in range(3):
        total = total + r1b[k].astype(F32)
    p2b[...] = total
    s2b[...] = total.astype(BF16)
    for k in (2, 1, 3):
        b2(k).start()

    lax.fori_loop(2, 3, finish, 0)

    for k in (1, 3, 2):
        a2(k).wait_recv()
    total = p2a[yy]
    for k in range(3):
        total = total + r2a[k].astype(F32)
    p3[:, :, :CA] = total.reshape(4, 8, CA)
    for k in (1, 3, 2):
        b2(k).wait_recv()
    total = p2b[z]
    for k in range(3):
        total = total + r2b[k].astype(F32)
    p3[:, :, CA:] = total.reshape(4, 8, CW - CA)
    for k in (2, 1, 3):
        x3(k).start()
    for k in (1, 3, 2):
        x3(k).wait_recv()
    total = p3[xx]
    for k in range(3):
        total = total + r3[k]
    gh_ref[...] = total[:, :1024]
    go_ref[...] = total[:, 1024:]

    lax.fori_loop(3, 4, finish, 0)

    for i in range(3):
        pred_copy(i).wait_send()
        for m in range(4):
            adj_copy(m, i).wait_send()
    for m in range(4):
        dn_copy(m).wait_send()
        up_copy(m).wait_send()
        c_copy(m).wait_send()
        out_copy(m).wait()
    for k in (1, 2, 3):
        for f in (a1, b1, a2, b2, x3):
            f(k).wait_send()


def body(
    grid_input, w_hidden, b_hidden, w_out, b_out, target, channel_weight, interp_weight, block_index
):
    V = pltpu.VMEM
    D = pltpu.SemaphoreType.DMA
    any_spec = pl.BlockSpec(memory_space=pl.ANY)
    vmem_spec = pl.BlockSpec(memory_space=pltpu.VMEM)
    scratch = [
        V((4, 4, 128, 1024), BF16), V((1024, 1024), BF16), V((96, 1024), BF16),
        V((4, 3, 128, 128), BF16), V((96, 128), F32),
        V((4, 4, 128, 1024), BF16), V((4, 4, 128, 1024), F32), V((4, 4, 128, 1024), BF16),
        V((4, 768, 128), BF16), V((128, 128), F32), V((128, 128), F32),
        V((4, 4, 96, 128), BF16), V((3, 4, 96, 128), BF16),
        V((16, 96, 128), F32), V((16, 96, 128), F32),
        V((4, 3, 96, 128), BF16), V((4, 4, 96, 128), BF16), V((128, 1024), F32),
        V((4, 256, 1024), F32),
        V((4, 256, 1024), BF16), V((4, 256, 1024), BF16),
        V((4, 256, 1024), BF16), V((4, 256, 1024), BF16),
        V((2, 4, 4, 32, CW), F32), V((4, 4, 32, CW), BF16), V((4, 4, 32, CW), BF16),
        V((4, 4, 32, CA), BF16), V((4, 4, 32, CW - CA), BF16),
        V((3, 4, 32, CA), BF16), V((3, 4, 32, CW - CA), BF16),
        V((4, 32, CA), F32), V((4, 32, CW - CA), F32),
        V((4, 32, CA), BF16), V((4, 32, CW - CA), BF16),
        V((3, 32, CA), BF16), V((3, 32, CW - CA), BF16),
        V((4, 8, CW), F32), V((3, 8, CW), F32),
        D((4,)), D((4,)), D((3,)), D((3,)), D((4, 3)), D((4, 3)),
        D((4,)), D((4,)), D((4,)), D((4,)), D((4,)), D((4,)),
        D((3,)), D((3,)), D((3,)), D((3,)), D((3,)), D((3,)), D((3,)), D((3,)),
        D((3,)), D((3,)), D((4,)),
    ]
    grad_hidden, grad_out, grad_mesh = pl.pallas_call(
        kernel,
        out_shape=(
            jax.ShapeDtypeStruct((8, 1024), F32),
            jax.ShapeDtypeStruct((8, 128), F32),
            jax.ShapeDtypeStruct((4, 256, 1024), F32),
        ),
        in_specs=[any_spec] * 3 + [vmem_spec] * 3 + [any_spec] * 2
        + [pl.BlockSpec(memory_space=pltpu.SMEM)],
        out_specs=(vmem_spec, vmem_spec, any_spec),
        scratch_shapes=scratch,
        compiler_params=pltpu.CompilerParams(
            collective_id=0, has_side_effects=True, vmem_limit_bytes=60 * 1024 * 1024
        ),
    )(
        grid_input, w_hidden, w_out.T, b_hidden[None], b_out[None], channel_weight[None],
        target, interp_weight, block_index,
    )
    return grad_hidden, grad_out[:, :96], grad_mesh


def solution(mesh):
    placed = (
        P("member", "region", None),
        P(),
        P(),
        P(),
        P(),
        P(None, "region"),
        P(),
        P("region", None, None, None),
        P("region", None),
    )
    return jax.shard_map(
        body,
        mesh=mesh,
        in_specs=placed,
        out_specs=(
            P(("member", "region"), None),
            P(("member", "region"), None),
            P("member", "region", None),
        ),
        check_vma=False,
    )
```

time: 379 us -> 77.4 us (0.20)
  waiting for transfers between devices: 186 us -> 0 us
  Pallas kernels: 0 us -> 69.1 us
  matrix products: 66.4 us -> 0 us
  local copies, waits for them, and re-layouts: 59.9 us -> 7.44 us
  loops' own time: 23.9 us -> 0 us
  other arithmetic: 14.4 us -> 0 us
  between operations: 14.2 us -> 0.64 us
  starting transfers between devices: 11.5 us -> 0 us
    unnamed x2 -> x0, waiting for transfers between devices: 165 us -> none
    pallas_call x0 -> x1, Pallas kernels: none -> 69.1 us  [body(): pl.pallas_call(kernel, out_shape=(jax.ShapeDtypeStruct((8, 1024), F32), j...]
    dot_general x18 -> x0, matrix products: 66.4 us -> none  [the longest x12 37 us: add_block(): jnp.einsum('gn,mgh->mnh', weight_tile, block_rows, preferred_element_type...]
    dynamic_slice x25 -> x0, local copies, waits for them, and re-layouts: 28.6 us -> none  [the longest x12 20.8 us: add_block(): current = lax.dynamic_index_in_dim(accum, target_slot, 1, False)]
    another operation x1 -> x0, loops' own time: 23.9 us -> none  [body(): buffer = lax.fori_loop(0, GBLK_REG * K, add_block, buffer)]
    all_to_all x2 -> x0, waiting for transfers between devices: 21.3 us -> none  [the longest x1 14.3 us: body(): lax.all_to_all(pred_cols, 'member', split_axis=2, concat_axis=0, tiled=True)]
    slice x4 -> x0, local copies, waits for them, and re-layouts: 9.41 us -> none  [the longest x1 4.77 us: body(): from_above = shifted(buffer[:, :MBLK_REG], 'region', -1)]
    all_to_all x2 -> x0, starting transfers between devices: 8.87 us -> none  [the longest x1 5.41 us: body(): lax.all_to_all(pred_cols, 'member', split_axis=2, concat_axis=0, tiled=True)]
  transfers between devices with their start and end apart: 5 -> 0, of which waited for: 3 -> 0; matrix products, arithmetic and copies ran while one was open for 4% -> 0% of each run, Pallas kernels for 0% -> 0%
where the time goes in v1:
time: 77.4 us; the launch traced here: 77.1 us
  Pallas kernels  69.1 us (89%)
  local copies, waits for them, and re-layouts  7.44 us (10%)
    pallas_call x1, Pallas kernels, body(): pl.pallas_call(kernel, out_shape=(jax.ShapeDtypeStruct((8, 1024), F32), j...  69.1 us
    unnamed x3, local copies, waits for them, and re-layouts  7.44 us

profile of v1, /device:TPU:0, one launch (start us, length us, event | category | flops | bytes accessed | tf_op | source)
XLA Modules:
  0.0 77.1 jit_solution(18060798660329192467)
XLA Ops:
  0.6 69.1 %shard_map.112 = (f32[8,1024]{1,0:T(8,128)}, f32[8,128]{1,0:T(8,128)}, f32[4,256,1024]{2,1,0:T(8,128)}) custom-call(bf16[4,512,1024]{2,1,0:T(8,128)(2,1)} %x_hbm.1, bf16[1024,1024]{1,0:T(8,128)(2,1)} %wh_hbm.1, bf16[96,1024]{1,0:T(8,128)(2,1)} %bitcast.5, f32[1,1024]{1,0:T(1,128)} %bitcast.6, f32[1,96]{1,0:T(1,128)} %bitcast.8, f32[1,96]{1,0:T(1,128)} %bitcast.9, ...), custom_call_target="tpu_custom_call" | custom-call | tf_op jit(solution)/shard_map/pallas_call | solution.py:391
  69.7 1.4 %copy.15 = f32[8,1024]{1,0:T(8,128)} copy(f32[8,1024]{1,0:T(8,128)} %get-tuple-element.12) | data formatting | bytes 65536
  71.1 1.3 %copy.16 = f32[8,96]{1,0:T(8,128)} copy(f32[8,96]{1,0:T(8,128)} %bitcast.7) | data formatting | bytes 6144
  72.4 4.8 %copy.17 = f32[4,256,1024]{2,1,0:T(8,128)} copy(f32[4,256,1024]{2,1,0:T(8,128)} %get-tuple-element.14) | data formatting | bytes 8388608

commit v2 on v1

--- a/solution.py
+++ b/solution.py
@@ -18,13 +18,13 @@
 
 def kernel(
     x_hbm, wh_hbm, wot_hbm, bh_ref, bo_ref, cw_ref, tgt_hbm, tile_hbm, bi_ref,
-    gh_ref, go_ref, mesh_hbm,
-    xv, wh, wot, tiles, tgt, act, dsil, dpre, wt, bcol, ccol,
+    gh_ref, go_ref, own,
+    xv, wh, wht, wot, wo, tiles, tgt, act, dsil, dpre, wt, bcol, ccol,
     predsend, predrecv, pf, adjf, adjsend, adjrecv, outt,
-    own, send_dn, send_up, recv_dn, recv_up,
+    send_dn, send_up, recv_dn, recv_up,
     accf, csend, crecv, s1a, s1b, r1a, r1b, p2a, p2b, s2a, s2b, r2a, r2b, p3, r3,
     load_sem, x_sem, pred_ss, pred_rs, adj_ss, adj_rs, dn_ss, dn_rs, up_ss, up_rs,
-    c_ss, c_rs, a1_ss, a1_rs, b1_ss, b1_rs, a2_ss, a2_rs, b2_ss, b2_rs, x_ss, x_rs, out_sem,
+    c_ss, c_rs, a1_ss, a1_rs, b1_ss, b1_rs, a2_ss, a2_rs, b2_ss, b2_rs, x_ss, x_rs,
 ):
     z = lax.axis_index("member")
     r = lax.axis_index("region")
@@ -47,6 +47,11 @@
     def block_of(i):
         return (z + 1 + i) % 4
 
+    barrier = pltpu.get_barrier_semaphore()
+    peers = [f(k) for f in (zdev, ydev, xdev) for k in (1, 2, 3)] + [up, down]
+    for peer in peers:
+        pl.semaphore_signal(barrier, inc=1, device_id=peer, device_id_type=MESH)
+
     load_wh = pltpu.make_async_copy(wh_hbm, wh, load_sem.at[0])
     load_wh.start()
 
@@ -57,7 +62,7 @@
         )
 
     x_copy(0).start()
-    load_wot = pltpu.make_async_copy(wot_hbm, wot, load_sem.at[1])
+    load_wot = pltpu.make_async_copy(wot_hbm, wot.at[:96], load_sem.at[1])
     load_wot.start()
     for i in range(1, 4):
         x_copy(i).start()
@@ -68,12 +73,6 @@
     )
     load_tgt.start()
 
-    barrier = pltpu.get_barrier_semaphore()
-    peers = [f(k) for f in (zdev, ydev, xdev) for k in (1, 2, 3)] + [up, down]
-    for peer in peers:
-        pl.semaphore_signal(barrier, inc=1, device_id=peer, device_id_type=MESH)
-    pl.semaphore_wait(barrier, len(peers))
-
     def pred_copy(i):
         return pltpu.make_async_remote_copy(
             src_ref=predsend.at[i], dst_ref=predrecv.at[i],
@@ -81,8 +80,10 @@
             device_id=zdev(i + 1), device_id_type=MESH,
         )
 
+    wot[96:] = jnp.zeros((32, 1024), BF16)
+    load_wot.wait()
+    wo[...] = wot[...].T
     load_wh.wait()
-    load_wot.wait()
 
     def forward(i, carry):
         x_copy(i).wait()
@@ -94,12 +95,15 @@
             silu = pre * sig
             act[i, :, :, cols] = silu.astype(BF16).reshape(4, 128, 256)
             dsil[i, :, :, cols] = (sig + silu * (1.0 - sig)).reshape(4, 128, 256)
-        predt = lax.dot_general(
-            wot[...], act[i].reshape(512, 1024), (((1,), (1,)), ((), ())),
-            preferred_element_type=F32,
-        ).astype(BF16)
+        predt = jnp.dot(
+            act[i].reshape(512, 1024), wo[...], preferred_element_type=F32
+        ).T.astype(BF16)
         for m in range(4):
-            predsend[i, m] = predt[:, m * 128 : m * 128 + 128]
+            predsend[i, m] = predt[:96, m * 128 : m * 128 + 128]
+
+        @pl.when(i == 0)
+        def _():
+            pl.semaphore_wait(barrier, len(peers))
 
         @pl.when(i < 3)
         def _():
@@ -113,6 +117,7 @@
 
     def build(i, carry):
         b = block_of(i)
+        place = pl.ds(pl.multiple_of(i * 128, 128), 128)
         slots = []
         turned = []
         for k in range(3):
@@ -125,10 +130,13 @@
             for k in range(3):
                 term = turned[k] * jnp.where(slots[k] == s, 1.0, 0.0)
                 total = term if total is None else total + term
-            wt[i, s * 128 : s * 128 + 128, :] = total.astype(BF16)
+            wt[s * 128 : s * 128 + 128, place] = total.astype(BF16)
         return carry
 
     lax.fori_loop(0, 4, build, 0)
+
+    for n in range(4):
+        wht[:, n * 256 : n * 256 + 256] = wh[n * 256 : n * 256 + 256, :].T
 
     bcol[...] = jnp.zeros_like(bcol)
     ccol[...] = jnp.zeros_like(ccol)
@@ -193,36 +201,44 @@
 
     outt[...] = jnp.zeros_like(outt)
 
-    def backward(m, carry):
+    def hidden(m):
         for i in range(3):
             adj_copy(m, i).wait_recv()
         adj = jnp.concatenate([adjrecv[m, i] for i in range(4)], axis=1)
         for n in range(4):
             cols = slice(n * 256, n * 256 + 256)
             dact = lax.dot_general(
-                adj, wot[:, cols], (((0,), (0,)), ((), ())), preferred_element_type=F32
+                adj, wot[:96, cols], (((0,), (0,)), ((), ())), preferred_element_type=F32
             )
             grad = dact * dsil[:, m, :, cols].reshape(512, 256)
             dpre[:, m, :, cols] = grad.astype(BF16).reshape(4, 128, 256)
         outt[:96, :] += jnp.dot(
             adj, act[:, m].reshape(512, 1024), preferred_element_type=F32
         )
+
+    def interpolate(m):
         dp = dpre[:, m].reshape(512, 1024)
-        lhs = jnp.concatenate([wt[i] for i in range(4)], axis=1)
         for n in range(4):
             cols = slice(n * 256, n * 256 + 256)
-            dinput = lax.dot_general(
-                dp, wh[cols, :], (((1,), (1,)), ((), ())), preferred_element_type=F32
-            ).astype(BF16)
-            contrib = jnp.dot(lhs, dinput, preferred_element_type=F32)
+            dinput = jnp.dot(dp, wht[:, cols], preferred_element_type=F32).astype(BF16)
+            contrib = jnp.dot(wt[...], dinput, preferred_element_type=F32)
             send_dn[m, :, cols] = contrib[:256].astype(BF16)
             own[m, :, cols] = contrib[256:512]
             send_up[m, :, cols] = contrib[512:].astype(BF16)
         dn_copy(m).start()
         up_copy(m).start()
-        return carry
-
-    lax.fori_loop(0, 4, backward, 0)
+
+    def first_half(m, carry):
+        hidden(m)
+        interpolate(m)
+        return carry
+
+    def second_half(m, carry):
+        hidden(m)
+        return carry
+
+    lax.fori_loop(0, 2, first_half, 0)
+    lax.fori_loop(2, 4, second_half, 0)
 
     turned_out = outt[...].T.reshape(4, 4, 4, 2, 8, 128)
     for c in range(2):
@@ -260,8 +276,6 @@
         s1b[:, zc] = total[:, :, CA:].astype(BF16)
         return carry
 
-    lax.fori_loop(0, 4, combine, 0)
-
     def remote(src, dst, ss, rs, dev, k):
         return pltpu.make_async_remote_copy(
             src_ref=src, dst_ref=dst, send_sem=ss.at[k - 1], recv_sem=rs.at[k - 1],
@@ -283,21 +297,25 @@
     def x3(k):
         return remote(p3.at[(xx + k) % 4], r3.at[k - 1], x_ss, x_rs, xdev(k), k)
 
-    for k in (2, 1, 3):
-        a1(k).start()
-        b1(k).start()
-
-    def out_copy(m):
-        return pltpu.make_async_copy(own.at[m], mesh_hbm.at[m], out_sem.at[m])
+    def last(m, carry):
+        interpolate(m)
+
+        @pl.when(m == 2)
+        def _():
+            lax.fori_loop(0, 4, combine, 0)
+            for k in (2, 1, 3):
+                a1(k).start()
+                b1(k).start()
+
+        return carry
+
+    lax.fori_loop(2, 4, last, 0)
 
     def finish(m, carry):
         dn_copy(m).wait_recv()
         up_copy(m).wait_recv()
         own[m] = own[m] + recv_dn[m].astype(F32) + recv_up[m].astype(F32)
-        out_copy(m).start()
-        return carry
-
-    lax.fori_loop(0, 2, finish, 0)
+        return carry
 
     for k in (1, 3, 2):
         a1(k).wait_recv()
@@ -318,7 +336,7 @@
     for k in (2, 1, 3):
         b2(k).start()
 
-    lax.fori_loop(2, 3, finish, 0)
+    lax.fori_loop(0, 2, finish, 0)
 
     for k in (1, 3, 2):
         a2(k).wait_recv()
@@ -334,6 +352,8 @@
     p3[:, :, CA:] = total.reshape(4, 8, CW - CA)
     for k in (2, 1, 3):
         x3(k).start()
+    lax.fori_loop(2, 3, finish, 0)
+
     for k in (1, 3, 2):
         x3(k).wait_recv()
     total = p3[xx]
@@ -352,10 +372,19 @@
         dn_copy(m).wait_send()
         up_copy(m).wait_send()
         c_copy(m).wait_send()
-        out_copy(m).wait()
     for k in (1, 2, 3):
         for f in (a1, b1, a2, b2, x3):
             f(k).wait_send()
+
+
+def store(gh_ref, go_ref, mesh_ref, gh_out, go_out, mesh_out, sem):
+    copies = [pltpu.make_async_copy(mesh_ref.at[m], mesh_out.at[m], sem.at[m]) for m in range(4)]
+    for copy in copies:
+        copy.start()
+    gh_out[...] = gh_ref[...]
+    go_out[...] = go_ref[:, :96]
+    for copy in copies:
+        copy.wait()
 
 
 def body(
@@ -366,14 +395,14 @@
     any_spec = pl.BlockSpec(memory_space=pl.ANY)
     vmem_spec = pl.BlockSpec(memory_space=pltpu.VMEM)
     scratch = [
-        V((4, 4, 128, 1024), BF16), V((1024, 1024), BF16), V((96, 1024), BF16),
+        V((4, 4, 128, 1024), BF16), V((1024, 1024), BF16), V((1024, 1024), BF16),
+        V((128, 1024), BF16), V((1024, 128), BF16),
         V((4, 3, 128, 128), BF16), V((96, 128), F32),
         V((4, 4, 128, 1024), BF16), V((4, 4, 128, 1024), F32), V((4, 4, 128, 1024), BF16),
-        V((4, 768, 128), BF16), V((128, 128), F32), V((128, 128), F32),
+        V((768, 512), BF16), V((128, 128), F32), V((128, 128), F32),
         V((4, 4, 96, 128), BF16), V((3, 4, 96, 128), BF16),
         V((16, 96, 128), F32), V((16, 96, 128), F32),
         V((4, 3, 96, 128), BF16), V((4, 4, 96, 128), BF16), V((128, 1024), F32),
-        V((4, 256, 1024), F32),
         V((4, 256, 1024), BF16), V((4, 256, 1024), BF16),
         V((4, 256, 1024), BF16), V((4, 256, 1024), BF16),
         V((2, 4, 4, 32, CW), F32), V((4, 4, 32, CW), BF16), V((4, 4, 32, CW), BF16),
@@ -386,27 +415,35 @@
         D((4,)), D((4,)), D((3,)), D((3,)), D((4, 3)), D((4, 3)),
         D((4,)), D((4,)), D((4,)), D((4,)), D((4,)), D((4,)),
         D((3,)), D((3,)), D((3,)), D((3,)), D((3,)), D((3,)), D((3,)), D((3,)),
-        D((3,)), D((3,)), D((4,)),
+        D((3,)), D((3,)),
     ]
-    grad_hidden, grad_out, grad_mesh = pl.pallas_call(
+    held = pl.pallas_call(
         kernel,
-        out_shape=(
-            jax.ShapeDtypeStruct((8, 1024), F32),
-            jax.ShapeDtypeStruct((8, 128), F32),
-            jax.ShapeDtypeStruct((4, 256, 1024), F32),
-        ),
+        out_shape=(V((8, 1024), F32), V((8, 128), F32), V((4, 256, 1024), F32)),
         in_specs=[any_spec] * 3 + [vmem_spec] * 3 + [any_spec] * 2
         + [pl.BlockSpec(memory_space=pltpu.SMEM)],
-        out_specs=(vmem_spec, vmem_spec, any_spec),
+        out_specs=(vmem_spec, vmem_spec, vmem_spec),
         scratch_shapes=scratch,
         compiler_params=pltpu.CompilerParams(
-            collective_id=0, has_side_effects=True, vmem_limit_bytes=60 * 1024 * 1024
+            collective_id=0, has_side_effects=True, vmem_limit_bytes=54 * 2**20
         ),
     )(
         grid_input, w_hidden, w_out.T, b_hidden[None], b_out[None], channel_weight[None],
         target, interp_weight, block_index,
     )
-    return grad_hidden, grad_out[:, :96], grad_mesh
+    held = [pltpu.with_memory_space_constraint(h, pltpu.VMEM) for h in held]
+    return pl.pallas_call(
+        store,
+        out_shape=(
+            jax.ShapeDtypeStruct((8, 1024), F32),
+            jax.ShapeDtypeStruct((8, 96), F32),
+            jax.ShapeDtypeStruct((4, 256, 1024), F32),
+        ),
+        in_specs=[vmem_spec] * 3,
+        out_specs=(vmem_spec, vmem_spec, any_spec),
+        scratch_shapes=[D((4,))],
+        compiler_params=pltpu.CompilerParams(vmem_limit_bytes=2**20),
+    )(*held)
 
 
 def solution(mesh):

time: 77.4 us -> 74.3 us (0.960)
  local copies, waits for them, and re-layouts: 7.44 us -> 0 us
  Pallas kernels: 69.1 us -> 73.5 us
    unnamed x3 -> x0, local copies, waits for them, and re-layouts: 7.44 us -> none
    pallas_call x1 -> x2, Pallas kernels: 69.1 us -> 73.5 us  [the longest x1 70.8 us: body(): pl.pallas_call(kernel, out_shape=(V((8, 1024), F32), V((8, 128), F32), V(...]
where the time goes in v2:
time: 74.3 us; the launch traced here: 74.1 us
  Pallas kernels  73.5 us (99%)
    pallas_call x1, Pallas kernels, body(): pl.pallas_call(kernel, out_shape=(V((8, 1024), F32), V((8, 128), F32), V(...  70.8 us
    pallas_call x1, Pallas kernels, body(): pl.pallas_call(store, out_shape=(jax.ShapeDtypeStruct((8, 1024), F32), ja...  2.66 us

profile of v2, /device:TPU:0, one launch (start us, length us, event | category | flops | bytes accessed | tf_op | source)
XLA Modules:
  0.0 74.1 jit_solution(10726658212937593222)
XLA Ops:
  0.6 70.8 %shard_map.112 = (f32[8,1024]{1,0:T(8,128)S(1)}, f32[8,128]{1,0:T(8,128)S(1)}, f32[4,256,1024]{2,1,0:T(8,128)S(1)}) custom-call(bf16[4,512,1024]{2,1,0:T(8,128)(2,1)} %x_hbm.1, bf16[1024,1024]{1,0:T(8,128)(2,1)} %wh_hbm.1, bf16[96,1024]{1,0:T(8,128)(2,1)} %bitcast.4, f32[1,1024]{1,0:T(1,128)} %bitcast.5, f32[1,96]{1,0:T(1,128)} %bitcast.6, f32[1,96]{1,0:T(1,128)} %bitcast.7, ...), custom_call_target="tpu_custom_call" | custom-call | tf_op jit(solution)/shard_map/pallas_call | solution.py:420
  71.5 2.7 %shard_map.113 = (f32[8,1024]{1,0:T(8,128)}, f32[8,96]{1,0:T(8,128)}, f32[4,256,1024]{2,1,0:T(8,128)}) custom-call(f32[8,1024]{1,0:T(8,128)S(1)} %get-tuple-element.6.gh_ref, f32[8,128]{1,0:T(8,128)S(1)} %get-tuple-element.7.go_ref, f32[4,256,1024]{2,1,0:T(8,128)S(1)} %get-tuple-element.8.mesh_ref), custom_call_target="tpu_custom_call" | custom-call | tf_op jit(solution)/shard_map/pallas_call | solution.py:435

commit v3 on v2

--- a/solution.py
+++ b/solution.py
@@ -19,10 +19,10 @@
 def kernel(
     x_hbm, wh_hbm, wot_hbm, bh_ref, bo_ref, cw_ref, tgt_hbm, tile_hbm, bi_ref,
     gh_ref, go_ref, own,
-    xv, wh, wht, wot, wo, tiles, tgt, act, dsil, dpre, wt, bcol, ccol,
+    xv, wh, wht, wot, tiles, tgt, act, dsil, dpre, wt, bcol, ccol,
     predsend, predrecv, pf, adjf, adjsend, adjrecv, outt,
     send_dn, send_up, recv_dn, recv_up,
-    accf, csend, crecv, s1a, s1b, r1a, r1b, p2a, p2b, s2a, s2b, r2a, r2b, p3, r3,
+    accf, csend, crecv, s1a, s1b, ra, rb, p2a, p2b, s2a, s2b, r2a, r2b, p3, r3,
     load_sem, x_sem, pred_ss, pred_rs, adj_ss, adj_rs, dn_ss, dn_rs, up_ss, up_rs,
     c_ss, c_rs, a1_ss, a1_rs, b1_ss, b1_rs, a2_ss, a2_rs, b2_ss, b2_rs, x_ss, x_rs,
 ):
@@ -62,7 +62,7 @@
         )
 
     x_copy(0).start()
-    load_wot = pltpu.make_async_copy(wot_hbm, wot.at[:96], load_sem.at[1])
+    load_wot = pltpu.make_async_copy(wot_hbm, wot, load_sem.at[1])
     load_wot.start()
     for i in range(1, 4):
         x_copy(i).start()
@@ -80,9 +80,7 @@
             device_id=zdev(i + 1), device_id_type=MESH,
         )
 
-    wot[96:] = jnp.zeros((32, 1024), BF16)
     load_wot.wait()
-    wo[...] = wot[...].T
     load_wh.wait()
 
     def forward(i, carry):
@@ -95,11 +93,12 @@
             silu = pre * sig
             act[i, :, :, cols] = silu.astype(BF16).reshape(4, 128, 256)
             dsil[i, :, :, cols] = (sig + silu * (1.0 - sig)).reshape(4, 128, 256)
-        predt = jnp.dot(
-            act[i].reshape(512, 1024), wo[...], preferred_element_type=F32
-        ).T.astype(BF16)
+        predt = lax.dot_general(
+            wot[...], act[i].reshape(512, 1024), (((1,), (1,)), ((), ())),
+            preferred_element_type=F32,
+        ).astype(BF16)
         for m in range(4):
-            predsend[i, m] = predt[:96, m * 128 : m * 128 + 128]
+            predsend[i, m] = predt[:, m * 128 : m * 128 + 128]
 
         @pl.when(i == 0)
         def _():
@@ -208,7 +207,7 @@
         for n in range(4):
             cols = slice(n * 256, n * 256 + 256)
             dact = lax.dot_general(
-                adj, wot[:96, cols], (((0,), (0,)), ((), ())), preferred_element_type=F32
+                adj, wot[:, cols], (((0,), (0,)), ((), ())), preferred_element_type=F32
             )
             grad = dact * dsil[:, m, :, cols].reshape(512, 256)
             dpre[:, m, :, cols] = grad.astype(BF16).reshape(4, 128, 256)
@@ -218,13 +217,11 @@
 
     def interpolate(m):
         dp = dpre[:, m].reshape(512, 1024)
-        for n in range(4):
-            cols = slice(n * 256, n * 256 + 256)
-            dinput = jnp.dot(dp, wht[:, cols], preferred_element_type=F32).astype(BF16)
-            contrib = jnp.dot(wt[...], dinput, preferred_element_type=F32)
-            send_dn[m, :, cols] = contrib[:256].astype(BF16)
-            own[m, :, cols] = contrib[256:512]
-            send_up[m, :, cols] = contrib[512:].astype(BF16)
+        dinput = jnp.dot(dp, wht[...], preferred_element_type=F32).astype(BF16)
+        contrib = jnp.dot(wt[...], dinput, preferred_element_type=F32)
+        send_dn[m] = contrib[:256].astype(BF16)
+        own[m] = contrib[256:512]
+        send_up[m] = contrib[512:].astype(BF16)
         dn_copy(m).start()
         up_copy(m).start()
 
@@ -282,11 +279,60 @@
             device_id=dev, device_id_type=MESH,
         )
 
-    def a1(k):
-        return remote(s1a.at[(z + k) % 4], r1a.at[k - 1], a1_ss, a1_rs, zdev(k), k)
-
-    def b1(k):
-        return remote(s1b.at[(yy + k) % 4], r1b.at[k - 1], b1_ss, b1_rs, ydev(k), k)
+    def ring(dev, me, s1, relay, direct, onward, summed, get, ss, rs):
+        after, before, far = (me + 1) % 4, (me + 3) % 4, (me + 2) % 4
+        low, high = slice(0, 2), slice(2, 4)
+
+        def copy(n):
+            src, dst, k = (
+                (s1.at[far, low], relay.at[0], 1),
+                (s1.at[far, high], relay.at[1], 3),
+                (s1.at[after, high], direct.at[0], 1),
+                (s1.at[before, low], direct.at[1], 3),
+                (onward.at[0], summed.at[0], 1),
+                (onward.at[1], summed.at[1], 3),
+            )[n]
+            return pltpu.make_async_remote_copy(
+                src_ref=src, dst_ref=dst, send_sem=ss.at[n], recv_sem=rs.at[n],
+                device_id=dev(k), device_id_type=MESH,
+            )
+
+        def begin():
+            for n in range(4):
+                copy(n).start()
+
+        def pass_on():
+            copy(0).wait_recv()
+            onward[0] = (get(after, low) + relay[0].astype(F32)).astype(BF16)
+            copy(4).start()
+            copy(1).wait_recv()
+            onward[1] = (get(before, high) + relay[1].astype(F32)).astype(BF16)
+            copy(5).start()
+
+        def end(out, out16):
+            for n in range(2, 6):
+                copy(n).wait_recv()
+            first = get(me, low) + summed[0].astype(F32) + direct[1].astype(F32)
+            second = get(me, high) + summed[1].astype(F32) + direct[0].astype(F32)
+            out[0:2] = first
+            out[2:4] = second
+            out16[0:2] = first.astype(BF16)
+            out16[2:4] = second.astype(BF16)
+
+        def sent():
+            for n in range(6):
+                copy(n).wait_send()
+
+        return begin, pass_on, end, sent
+
+    ring_a = ring(
+        zdev, z, s1a, ra.at[0], ra.at[1], ra.at[2], ra.at[3],
+        lambda j, part: accf[cc, j, part, :, :CA], a1_ss, a1_rs,
+    )
+    ring_b = ring(
+        ydev, yy, s1b, rb.at[0], rb.at[1], rb.at[2], rb.at[3],
+        lambda j, part: accf[cc, part, j, :, CA:], b1_ss, b1_rs,
+    )
 
     def a2(k):
         return remote(s2a.at[(yy + k) % 4], r2a.at[k - 1], a2_ss, a2_rs, ydev(k), k)
@@ -303,9 +349,8 @@
         @pl.when(m == 2)
         def _():
             lax.fori_loop(0, 4, combine, 0)
-            for k in (2, 1, 3):
-                a1(k).start()
-                b1(k).start()
+            ring_a[0]()
+            ring_b[0]()
 
         return carry
 
@@ -317,26 +362,17 @@
         own[m] = own[m] + recv_dn[m].astype(F32) + recv_up[m].astype(F32)
         return carry
 
-    for k in (1, 3, 2):
-        a1(k).wait_recv()
-    total = accf[cc, z, :, :, :CA]
-    for k in range(3):
-        total = total + r1a[k].astype(F32)
-    p2a[...] = total
-    s2a[...] = total.astype(BF16)
+    ring_a[1]()
+    ring_b[1]()
+    lax.fori_loop(0, 1, finish, 0)
+    ring_a[2](p2a, s2a)
     for k in (2, 1, 3):
         a2(k).start()
-    for k in (1, 3, 2):
-        b1(k).wait_recv()
-    total = accf[cc, :, yy, :, CA:]
-    for k in range(3):
-        total = total + r1b[k].astype(F32)
-    p2b[...] = total
-    s2b[...] = total.astype(BF16)
+    ring_b[2](p2b, s2b)
     for k in (2, 1, 3):
         b2(k).start()
 
-    lax.fori_loop(0, 2, finish, 0)
+    lax.fori_loop(1, 2, finish, 0)
 
     for k in (1, 3, 2):
         a2(k).wait_recv()
@@ -373,8 +409,10 @@
         up_copy(m).wait_send()
         c_copy(m).wait_send()
     for k in (1, 2, 3):
-        for f in (a1, b1, a2, b2, x3):
+        for f in (a2, b2, x3):
             f(k).wait_send()
+    ring_a[3]()
+    ring_b[3]()
 
 
 def store(gh_ref, go_ref, mesh_ref, gh_out, go_out, mesh_out, sem):
@@ -396,7 +434,7 @@
     vmem_spec = pl.BlockSpec(memory_space=pltpu.VMEM)
     scratch = [
         V((4, 4, 128, 1024), BF16), V((1024, 1024), BF16), V((1024, 1024), BF16),
-        V((128, 1024), BF16), V((1024, 128), BF16),
+        V((96, 1024), BF16),
         V((4, 3, 128, 128), BF16), V((96, 128), F32),
         V((4, 4, 128, 1024), BF16), V((4, 4, 128, 1024), F32), V((4, 4, 128, 1024), BF16),
         V((768, 512), BF16), V((128, 128), F32), V((128, 128), F32),
@@ -407,14 +445,14 @@
         V((4, 256, 1024), BF16), V((4, 256, 1024), BF16),
         V((2, 4, 4, 32, CW), F32), V((4, 4, 32, CW), BF16), V((4, 4, 32, CW), BF16),
         V((4, 4, 32, CA), BF16), V((4, 4, 32, CW - CA), BF16),
-        V((3, 4, 32, CA), BF16), V((3, 4, 32, CW - CA), BF16),
+        V((4, 2, 2, 32, CA), BF16), V((4, 2, 2, 32, CW - CA), BF16),
         V((4, 32, CA), F32), V((4, 32, CW - CA), F32),
         V((4, 32, CA), BF16), V((4, 32, CW - CA), BF16),
         V((3, 32, CA), BF16), V((3, 32, CW - CA), BF16),
         V((4, 8, CW), F32), V((3, 8, CW), F32),
         D((4,)), D((4,)), D((3,)), D((3,)), D((4, 3)), D((4, 3)),
         D((4,)), D((4,)), D((4,)), D((4,)), D((4,)), D((4,)),
-        D((3,)), D((3,)), D((3,)), D((3,)), D((3,)), D((3,)), D((3,)), D((3,)),
+        D((6,)), D((6,)), D((6,)), D((6,)), D((3,)), D((3,)), D((3,)), D((3,)),
         D((3,)), D((3,)),
     ]
     held = pl.pallas_call(

time: 74.3 us -> 69 us (0.929)
  Pallas kernels: 73.5 us -> 68.1 us
    pallas_call x1, Pallas kernels: 70.8 us -> 65.5 us  [body(): pl.pallas_call(kernel, out_shape=(V((8, 1024), F32), V((8, 128), F32), V(...]
where the time goes in v3:
time: 69 us; the launch traced here: 68.8 us
  Pallas kernels  68.1 us (99%)
    pallas_call x1, Pallas kernels, body(): pl.pallas_call(kernel, out_shape=(V((8, 1024), F32), V((8, 128), F32), V(...  65.5 us
    pallas_call x1, Pallas kernels, body(): pl.pallas_call(store, out_shape=(jax.ShapeDtypeStruct((8, 1024), F32), ja...  2.66 us

profile of v3, /device:TPU:0, one launch (start us, length us, event | category | flops | bytes accessed | tf_op | source)
XLA Modules:
  0.0 68.8 jit_solution(11287912248365038766)
XLA Ops:
  0.6 65.5 %shard_map.112 = (f32[8,1024]{1,0:T(8,128)S(1)}, f32[8,128]{1,0:T(8,128)S(1)}, f32[4,256,1024]{2,1,0:T(8,128)S(1)}) custom-call(bf16[4,512,1024]{2,1,0:T(8,128)(2,1)} %x_hbm.1, bf16[1024,1024]{1,0:T(8,128)(2,1)} %wh_hbm.1, bf16[96,1024]{1,0:T(8,128)(2,1)} %bitcast.4, f32[1,1024]{1,0:T(1,128)} %bitcast.5, f32[1,96]{1,0:T(1,128)} %bitcast.6, f32[1,96]{1,0:T(1,128)} %bitcast.7, ...), custom_call_target="tpu_custom_call" | custom-call | tf_op jit(solution)/shard_map/pallas_call | solution.py:458
  66.1 2.7 %shard_map.113 = (f32[8,1024]{1,0:T(8,128)}, f32[8,96]{1,0:T(8,128)}, f32[4,256,1024]{2,1,0:T(8,128)}) custom-call(f32[8,1024]{1,0:T(8,128)S(1)} %get-tuple-element.6.gh_ref, f32[8,128]{1,0:T(8,128)S(1)} %get-tuple-element.7.go_ref, f32[4,256,1024]{2,1,0:T(8,128)S(1)} %get-tuple-element.8.mesh_ref), custom_call_target="tpu_custom_call" | custom-call | tf_op jit(solution)/shard_map/pallas_call | solution.py:473

commit v4 on v2

--- a/solution.py
+++ b/solution.py
@@ -12,19 +12,18 @@
 ALPHA = 0.95
 SMOOTH = 0.25
 KAPPA = ALPHA / (2.0 * M * (M - 1)) + (1.0 - ALPHA) / (2.0 * M * M)
-CA = 640
 CW = 1152
 
 
 def kernel(
     x_hbm, wh_hbm, wot_hbm, bh_ref, bo_ref, cw_ref, tgt_hbm, tile_hbm, bi_ref,
     gh_ref, go_ref, own,
-    xv, wh, wht, wot, wo, tiles, tgt, act, dsil, dpre, wt, bcol, ccol,
+    xv, wh, wht, wot, tiles, tgt, act, dsil, dpre, wt, bcol, ccol,
     predsend, predrecv, pf, adjf, adjsend, adjrecv, outt,
     send_dn, send_up, recv_dn, recv_up,
-    accf, csend, crecv, s1a, s1b, r1a, r1b, p2a, p2b, s2a, s2b, r2a, r2b, p3, r3,
+    accf, csend, crecv, s1, ring_in, onward, p2, s2, r2, p3, r3,
     load_sem, x_sem, pred_ss, pred_rs, adj_ss, adj_rs, dn_ss, dn_rs, up_ss, up_rs,
-    c_ss, c_rs, a1_ss, a1_rs, b1_ss, b1_rs, a2_ss, a2_rs, b2_ss, b2_rs, x_ss, x_rs,
+    c_ss, c_rs, ring_ss, ring_rs, y_ss, y_rs, x_ss, x_rs,
 ):
     z = lax.axis_index("member")
     r = lax.axis_index("region")
@@ -62,7 +61,7 @@
         )
 
     x_copy(0).start()
-    load_wot = pltpu.make_async_copy(wot_hbm, wot.at[:96], load_sem.at[1])
+    load_wot = pltpu.make_async_copy(wot_hbm, wot, load_sem.at[1])
     load_wot.start()
     for i in range(1, 4):
         x_copy(i).start()
@@ -80,9 +79,7 @@
             device_id=zdev(i + 1), device_id_type=MESH,
         )
 
-    wot[96:] = jnp.zeros((32, 1024), BF16)
     load_wot.wait()
-    wo[...] = wot[...].T
     load_wh.wait()
 
     def forward(i, carry):
@@ -95,19 +92,22 @@
             silu = pre * sig
             act[i, :, :, cols] = silu.astype(BF16).reshape(4, 128, 256)
             dsil[i, :, :, cols] = (sig + silu * (1.0 - sig)).reshape(4, 128, 256)
-        predt = jnp.dot(
-            act[i].reshape(512, 1024), wo[...], preferred_element_type=F32
-        ).T.astype(BF16)
+        predt = lax.dot_general(
+            wot[...], act[i].reshape(512, 1024), (((1,), (1,)), ((), ())),
+            preferred_element_type=F32,
+        ).astype(BF16)
         for m in range(4):
-            predsend[i, m] = predt[:96, m * 128 : m * 128 + 128]
-
-        @pl.when(i == 0)
+            predsend[i, m] = predt[:, m * 128 : m * 128 + 128]
+
+        @pl.when(i == 1)
         def _():
             pl.semaphore_wait(barrier, len(peers))
-
-        @pl.when(i < 3)
+            pred_copy(0).start()
+            pred_copy(1).start()
+
+        @pl.when(i == 2)
         def _():
-            pred_copy(i).start()
+            pred_copy(2).start()
 
         return carry
 
@@ -135,9 +135,6 @@
 
     lax.fori_loop(0, 4, build, 0)
 
-    for n in range(4):
-        wht[:, n * 256 : n * 256 + 256] = wh[n * 256 : n * 256 + 256, :].T
-
     bcol[...] = jnp.zeros_like(bcol)
     ccol[...] = jnp.zeros_like(ccol)
     bcol[:, :96] = jnp.broadcast_to(bo_ref[...], (128, 96))
@@ -185,21 +182,23 @@
             adj_copy(m, i).start()
         adjrecv[m, 3] = adjf[12 + m].astype(BF16)
 
-    def dn_copy(m):
-        return pltpu.make_async_remote_copy(
-            src_ref=send_dn.at[m], dst_ref=recv_dn.at[m],
-            send_sem=dn_ss.at[m], recv_sem=dn_rs.at[m],
+    def dn_copy(m, h):
+        return pltpu.make_async_remote_copy(
+            src_ref=send_dn.at[m, h], dst_ref=recv_dn.at[m, h],
+            send_sem=dn_ss.at[m, h], recv_sem=dn_rs.at[m, h],
             device_id=down, device_id_type=MESH,
         )
 
-    def up_copy(m):
-        return pltpu.make_async_remote_copy(
-            src_ref=send_up.at[m], dst_ref=recv_up.at[m],
-            send_sem=up_ss.at[m], recv_sem=up_rs.at[m],
+    def up_copy(m, h):
+        return pltpu.make_async_remote_copy(
+            src_ref=send_up.at[m, h], dst_ref=recv_up.at[m, h],
+            send_sem=up_ss.at[m, h], recv_sem=up_rs.at[m, h],
             device_id=up, device_id_type=MESH,
         )
 
     outt[...] = jnp.zeros_like(outt)
+    for n in range(4):
+        wht[:, n * 256 : n * 256 + 256] = wh[n * 256 : n * 256 + 256, :].T
 
     def hidden(m):
         for i in range(3):
@@ -208,7 +207,7 @@
         for n in range(4):
             cols = slice(n * 256, n * 256 + 256)
             dact = lax.dot_general(
-                adj, wot[:96, cols], (((0,), (0,)), ((), ())), preferred_element_type=F32
+                adj, wot[:, cols], (((0,), (0,)), ((), ())), preferred_element_type=F32
             )
             grad = dact * dsil[:, m, :, cols].reshape(512, 256)
             dpre[:, m, :, cols] = grad.astype(BF16).reshape(4, 128, 256)
@@ -218,15 +217,22 @@
 
     def interpolate(m):
         dp = dpre[:, m].reshape(512, 1024)
-        for n in range(4):
-            cols = slice(n * 256, n * 256 + 256)
+        for h in range(2):
+            cols = slice(h * 512, h * 512 + 512)
             dinput = jnp.dot(dp, wht[:, cols], preferred_element_type=F32).astype(BF16)
             contrib = jnp.dot(wt[...], dinput, preferred_element_type=F32)
-            send_dn[m, :, cols] = contrib[:256].astype(BF16)
+            send_dn[m, h] = contrib[:256].astype(BF16)
             own[m, :, cols] = contrib[256:512]
-            send_up[m, :, cols] = contrib[512:].astype(BF16)
-        dn_copy(m).start()
-        up_copy(m).start()
+            send_up[m, h] = contrib[512:].astype(BF16)
+            if h == 0:
+                dn_copy(m, h).start()
+                up_copy(m, h).start()
+            else:
+
+                @pl.when(m < 3)
+                def _():
+                    dn_copy(m, 1).start()
+                    up_copy(m, 1).start()
 
     def first_half(m, carry):
         hidden(m)
@@ -244,14 +250,18 @@
     for c in range(2):
         accf[c, :, :, :, 1024:] = turned_out[:, :, :, c].reshape(4, 4, 32, 128)
 
-    def c_copy(zc):
-        return pltpu.make_async_remote_copy(
-            src_ref=csend.at[zc], dst_ref=crecv.at[zc],
-            send_sem=c_ss.at[zc], recv_sem=c_rs.at[zc],
+    def row_of(j):
+        return (z + 2 + j + (j // 2) * (2 * j - 3)) % 4
+
+    def c_copy(j):
+        return pltpu.make_async_remote_copy(
+            src_ref=csend.at[j], dst_ref=crecv.at[j],
+            send_sem=c_ss.at[j], recv_sem=c_rs.at[j],
             device_id=partner, device_id_type=MESH,
         )
 
-    def weights(zc, carry):
+    def gradient(j):
+        zc = row_of(j)
         start = pl.multiple_of(zc * 256, 256)
         lhs = xv[:, :, :, pl.ds(start, 256)].reshape(2048, 256)
         for n in range(2):
@@ -262,19 +272,15 @@
             ).reshape(4, 4, 2, 8, 512)
             for c in range(2):
                 accf[c, zc, :, :, cols] = part[:, :, c].reshape(4, 32, 512)
-        csend[zc] = accf[oc, zc].astype(BF16)
-        c_copy(zc).start()
-        return carry
-
-    lax.fori_loop(0, 4, weights, 0)
-
-    def combine(zc, carry):
-        c_copy(zc).wait_recv()
-        total = accf[cc, zc] + crecv[zc].astype(F32)
+        csend[j] = accf[oc, zc].astype(BF16)
+        c_copy(j).start()
+
+    def combine(j):
+        zc = row_of(j)
+        c_copy(j).wait_recv()
+        total = accf[cc, zc] + crecv[j].astype(F32)
         accf[cc, zc] = total
-        s1a[zc] = total[:, :, :CA].astype(BF16)
-        s1b[:, zc] = total[:, :, CA:].astype(BF16)
-        return carry
+        s1[zc] = total.astype(BF16)
 
     def remote(src, dst, ss, rs, dev, k):
         return pltpu.make_async_remote_copy(
@@ -282,76 +288,104 @@
             device_id=dev, device_id_type=MESH,
         )
 
-    def a1(k):
-        return remote(s1a.at[(z + k) % 4], r1a.at[k - 1], a1_ss, a1_rs, zdev(k), k)
-
-    def b1(k):
-        return remote(s1b.at[(yy + k) % 4], r1b.at[k - 1], b1_ss, b1_rs, ydev(k), k)
-
-    def a2(k):
-        return remote(s2a.at[(yy + k) % 4], r2a.at[k - 1], a2_ss, a2_rs, ydev(k), k)
-
-    def b2(k):
-        return remote(s2b.at[(z + k) % 4], r2b.at[k - 1], b2_ss, b2_rs, zdev(k), k)
+    after, before, far = (z + 1) % 4, (z + 3) % 4, (z + 2) % 4
+    low, high = slice(0, 2), slice(2, 4)
+
+    def ring(n):
+        src, dst, k = (
+            (s1.at[far, low], ring_in.at[0], 1),
+            (s1.at[far, high], ring_in.at[1], 3),
+            (s1.at[after, high], ring_in.at[2], 1),
+            (s1.at[before, low], ring_in.at[3], 3),
+            (onward.at[0], ring_in.at[4], 1),
+            (onward.at[1], ring_in.at[5], 3),
+        )[n]
+        return pltpu.make_async_remote_copy(
+            src_ref=src, dst_ref=dst, send_sem=ring_ss.at[n], recv_sem=ring_rs.at[n],
+            device_id=zdev(k), device_id_type=MESH,
+        )
+
+    def y2(k):
+        return remote(s2.at[(yy + k) % 4], r2.at[k - 1], y_ss, y_rs, ydev(k), k)
 
     def x3(k):
         return remote(p3.at[(xx + k) % 4], r3.at[k - 1], x_ss, x_rs, xdev(k), k)
 
+    def weights(j, carry):
+        gradient(j)
+
+        @pl.when(j == 2)
+        def _():
+            combine(0)
+            ring(0).start()
+            ring(1).start()
+
+        @pl.when(j == 3)
+        def _():
+            combine(1)
+            ring(3).start()
+
+        return carry
+
+    lax.fori_loop(0, 4, weights, 0)
+
+    def pass_on():
+        ring(0).wait_recv()
+        onward[0] = (accf[cc, after, low] + ring_in[0].astype(F32)).astype(BF16)
+        ring(4).start()
+        ring(1).wait_recv()
+        onward[1] = (accf[cc, before, high] + ring_in[1].astype(F32)).astype(BF16)
+        ring(5).start()
+
+    combine(2)
+    ring(2).start()
+
     def last(m, carry):
         interpolate(m)
 
         @pl.when(m == 2)
         def _():
-            lax.fori_loop(0, 4, combine, 0)
-            for k in (2, 1, 3):
-                a1(k).start()
-                b1(k).start()
+            combine(3)
+            pass_on()
 
         return carry
 
     lax.fori_loop(2, 4, last, 0)
 
     def finish(m, carry):
-        dn_copy(m).wait_recv()
-        up_copy(m).wait_recv()
-        own[m] = own[m] + recv_dn[m].astype(F32) + recv_up[m].astype(F32)
-        return carry
+        for h in range(2):
+            cols = slice(h * 512, h * 512 + 512)
+            dn_copy(m, h).wait_recv()
+            up_copy(m, h).wait_recv()
+            own[m, :, cols] = (
+                own[m, :, cols] + recv_dn[m, h].astype(F32) + recv_up[m, h].astype(F32)
+            )
+        return carry
+
+    lax.fori_loop(0, 1, finish, 0)
+    for n in range(2, 6):
+        ring(n).wait_recv()
+    first = accf[cc, z, low] + ring_in[4].astype(F32) + ring_in[3].astype(F32)
+    second = accf[cc, z, high] + ring_in[5].astype(F32) + ring_in[2].astype(F32)
+    p2[0:2] = first
+    p2[2:4] = second
+    s2[0:2] = first.astype(BF16)
+    s2[2:4] = second.astype(BF16)
+    for k in (2, 1, 3):
+        y2(k).start()
+
+    lax.fori_loop(1, 2, finish, 0)
 
     for k in (1, 3, 2):
-        a1(k).wait_recv()
-    total = accf[cc, z, :, :, :CA]
+        y2(k).wait_recv()
+    total = p2[yy]
     for k in range(3):
-        total = total + r1a[k].astype(F32)
-    p2a[...] = total
-    s2a[...] = total.astype(BF16)
-    for k in (2, 1, 3):
-        a2(k).start()
-    for k in (1, 3, 2):
-        b1(k).wait_recv()
-    total = accf[cc, :, yy, :, CA:]
-    for k in range(3):
-        total = total + r1b[k].astype(F32)
-    p2b[...] = total
-    s2b[...] = total.astype(BF16)
-    for k in (2, 1, 3):
-        b2(k).start()
-
-    lax.fori_loop(0, 2, finish, 0)
-
-    for k in (1, 3, 2):
-        a2(k).wait_recv()
-    total = p2a[yy]
-    for k in range(3):
-        total = total + r2a[k].astype(F32)
-    p3[:, :, :CA] = total.reshape(4, 8, CA)
-    for k in (1, 3, 2):
-        b2(k).wait_recv()
-    total = p2b[z]
-    for k in range(3):
-        total = total + r2b[k].astype(F32)
-    p3[:, :, CA:] = total.reshape(4, 8, CW - CA)
+        total = total + r2[k].astype(F32)
+    p3[...] = total.reshape(4, 8, CW)
     for k in (2, 1, 3):
         x3(k).start()
+    dn_copy(3, 1).start()
+    up_copy(3, 1).start()
     lax.fori_loop(2, 3, finish, 0)
 
     for k in (1, 3, 2):
@@ -369,12 +403,15 @@
         for m in range(4):
             adj_copy(m, i).wait_send()
     for m in range(4):
-        dn_copy(m).wait_send()
-        up_copy(m).wait_send()
+        for h in range(2):
+            dn_copy(m, h).wait_send()
+            up_copy(m, h).wait_send()
         c_copy(m).wait_send()
     for k in (1, 2, 3):
-        for f in (a1, b1, a2, b2, x3):
+        for f in (y2, x3):
             f(k).wait_send()
+    for n in range(6):
+        ring(n).wait_send()
 
 
 def store(gh_ref, go_ref, mesh_ref, gh_out, go_out, mesh_out, sem):
@@ -396,26 +433,22 @@
     vmem_spec = pl.BlockSpec(memory_space=pltpu.VMEM)
     scratch = [
         V((4, 4, 128, 1024), BF16), V((1024, 1024), BF16), V((1024, 1024), BF16),
-        V((128, 1024), BF16), V((1024, 128), BF16),
+        V((96, 1024), BF16),
         V((4, 3, 128, 128), BF16), V((96, 128), F32),
         V((4, 4, 128, 1024), BF16), V((4, 4, 128, 1024), F32), V((4, 4, 128, 1024), BF16),
         V((768, 512), BF16), V((128, 128), F32), V((128, 128), F32),
         V((4, 4, 96, 128), BF16), V((3, 4, 96, 128), BF16),
         V((16, 96, 128), F32), V((16, 96, 128), F32),
         V((4, 3, 96, 128), BF16), V((4, 4, 96, 128), BF16), V((128, 1024), F32),
-        V((4, 256, 1024), BF16), V((4, 256, 1024), BF16),
-        V((4, 256, 1024), BF16), V((4, 256, 1024), BF16),
+        V((4, 2, 256, 512), BF16), V((4, 2, 256, 512), BF16),
+        V((4, 2, 256, 512), BF16), V((4, 2, 256, 512), BF16),
         V((2, 4, 4, 32, CW), F32), V((4, 4, 32, CW), BF16), V((4, 4, 32, CW), BF16),
-        V((4, 4, 32, CA), BF16), V((4, 4, 32, CW - CA), BF16),
-        V((3, 4, 32, CA), BF16), V((3, 4, 32, CW - CA), BF16),
-        V((4, 32, CA), F32), V((4, 32, CW - CA), F32),
-        V((4, 32, CA), BF16), V((4, 32, CW - CA), BF16),
-        V((3, 32, CA), BF16), V((3, 32, CW - CA), BF16),
+        V((4, 4, 32, CW), BF16), V((6, 2, 32, CW), BF16), V((2, 2, 32, CW), BF16),
+        V((4, 32, CW), F32), V((4, 32, CW), BF16), V((3, 32, CW), BF16),
         V((4, 8, CW), F32), V((3, 8, CW), F32),
         D((4,)), D((4,)), D((3,)), D((3,)), D((4, 3)), D((4, 3)),
-        D((4,)), D((4,)), D((4,)), D((4,)), D((4,)), D((4,)),
-        D((3,)), D((3,)), D((3,)), D((3,)), D((3,)), D((3,)), D((3,)), D((3,)),
-        D((3,)), D((3,)),
+        D((4, 2)), D((4, 2)), D((4, 2)), D((4, 2)), D((4,)), D((4,)),
+        D((6,)), D((6,)), D((3,)), D((3,)), D((3,)), D((3,)),
     ]
     held = pl.pallas_call(
         kernel,

time: 74.3 us -> 63.2 us (0.85)
  Pallas kernels: 73.5 us -> 61.9 us
    pallas_call x1, Pallas kernels: 70.8 us -> 59.2 us  [body(): pl.pallas_call(kernel, out_shape=(V((8, 1024), F32), V((8, 128), F32), V(...]
where the time goes in v4:
time: 63.2 us; the launch traced here: 62.5 us
  Pallas kernels  61.9 us (98%)
  between operations  0.64 us (1%)
    pallas_call x1, Pallas kernels, body(): pl.pallas_call(kernel, out_shape=(V((8, 1024), F32), V((8, 128), F32), V(...  59.2 us
    pallas_call x1, Pallas kernels, body(): pl.pallas_call(store, out_shape=(jax.ShapeDtypeStruct((8, 1024), F32), ja...  2.66 us

profile of v4, /device:TPU:0, one launch (start us, length us, event | category | flops | bytes accessed | tf_op | source)
XLA Modules:
  0.0 62.5 jit_solution(9995141738176060070)
XLA Ops:
  0.6 59.2 %shard_map.112 = (f32[8,1024]{1,0:T(8,128)S(1)}, f32[8,128]{1,0:T(8,128)S(1)}, f32[4,256,1024]{2,1,0:T(8,128)S(1)}) custom-call(bf16[4,512,1024]{2,1,0:T(8,128)(2,1)} %x_hbm.1, bf16[1024,1024]{1,0:T(8,128)(2,1)} %wh_hbm.1, bf16[96,1024]{1,0:T(8,128)(2,1)} %bitcast.4, f32[1,1024]{1,0:T(1,128)} %bitcast.5, f32[1,96]{1,0:T(1,128)} %bitcast.6, f32[1,96]{1,0:T(1,128)} %bitcast.7, ...), custom_call_target="tpu_custom_call" | custom-call | tf_op jit(solution)/shard_map/pallas_call | solution.py:453
  59.8 2.7 %shard_map.113 = (f32[8,1024]{1,0:T(8,128)}, f32[8,96]{1,0:T(8,128)}, f32[4,256,1024]{2,1,0:T(8,128)}) custom-call(f32[8,1024]{1,0:T(8,128)S(1)} %get-tuple-element.6.gh_ref, f32[8,128]{1,0:T(8,128)S(1)} %get-tuple-element.7.go_ref, f32[4,256,1024]{2,1,0:T(8,128)S(1)} %get-tuple-element.8.mesh_ref), custom_call_target="tpu_custom_call" | custom-call | tf_op jit(solution)/shard_map/pallas_call | solution.py:468

commit v5 on v4

--- a/solution.py
+++ b/solution.py
@@ -13,6 +13,7 @@
 SMOOTH = 0.25
 KAPPA = ALPHA / (2.0 * M * (M - 1)) + (1.0 - ALPHA) / (2.0 * M * M)
 CW = 1152
+PARTS = (slice(0, 640), slice(640, CW))
 
 
 def kernel(
@@ -21,7 +22,7 @@
     xv, wh, wht, wot, tiles, tgt, act, dsil, dpre, wt, bcol, ccol,
     predsend, predrecv, pf, adjf, adjsend, adjrecv, outt,
     send_dn, send_up, recv_dn, recv_up,
-    accf, csend, crecv, s1, ring_in, onward, p2, s2, r2, p3, r3,
+    accf, csend, crecv, s1, ring_in, onward, p2, s2, r2, p3, s3, r3,
     load_sem, x_sem, pred_ss, pred_rs, adj_ss, adj_rs, dn_ss, dn_rs, up_ss, up_rs,
     c_ss, c_rs, ring_ss, ring_rs, y_ss, y_rs, x_ss, x_rs,
 ):
@@ -99,15 +100,13 @@
         for m in range(4):
             predsend[i, m] = predt[:, m * 128 : m * 128 + 128]
 
-        @pl.when(i == 1)
+        @pl.when(i == 0)
         def _():
             pl.semaphore_wait(barrier, len(peers))
-            pred_copy(0).start()
-            pred_copy(1).start()
-
-        @pl.when(i == 2)
+
+        @pl.when(i < 3)
         def _():
-            pred_copy(2).start()
+            pred_copy(i).start()
 
         return carry
 
@@ -282,34 +281,37 @@
         accf[cc, zc] = total
         s1[zc] = total.astype(BF16)
 
-    def remote(src, dst, ss, rs, dev, k):
-        return pltpu.make_async_remote_copy(
-            src_ref=src, dst_ref=dst, send_sem=ss.at[k - 1], recv_sem=rs.at[k - 1],
-            device_id=dev, device_id_type=MESH,
-        )
-
     after, before, far = (z + 1) % 4, (z + 3) % 4, (z + 2) % 4
     low, high = slice(0, 2), slice(2, 4)
 
-    def ring(n):
+    def ring(n, h):
+        cols = PARTS[h]
         src, dst, k = (
-            (s1.at[far, low], ring_in.at[0], 1),
-            (s1.at[far, high], ring_in.at[1], 3),
-            (s1.at[after, high], ring_in.at[2], 1),
-            (s1.at[before, low], ring_in.at[3], 3),
-            (onward.at[0], ring_in.at[4], 1),
-            (onward.at[1], ring_in.at[5], 3),
+            (s1.at[far, low, :, cols], ring_in.at[0, :, :, cols], 1),
+            (s1.at[far, high, :, cols], ring_in.at[1, :, :, cols], 3),
+            (s1.at[after, high, :, cols], ring_in.at[2, :, :, cols], 1),
+            (s1.at[before, low, :, cols], ring_in.at[3, :, :, cols], 3),
+            (onward.at[0, :, :, cols], ring_in.at[4, :, :, cols], 1),
+            (onward.at[1, :, :, cols], ring_in.at[5, :, :, cols], 3),
         )[n]
         return pltpu.make_async_remote_copy(
-            src_ref=src, dst_ref=dst, send_sem=ring_ss.at[n], recv_sem=ring_rs.at[n],
+            src_ref=src, dst_ref=dst, send_sem=ring_ss.at[n, h], recv_sem=ring_rs.at[n, h],
             device_id=zdev(k), device_id_type=MESH,
         )
 
-    def y2(k):
-        return remote(s2.at[(yy + k) % 4], r2.at[k - 1], y_ss, y_rs, ydev(k), k)
-
-    def x3(k):
-        return remote(p3.at[(xx + k) % 4], r3.at[k - 1], x_ss, x_rs, xdev(k), k)
+    def y2(k, h):
+        return pltpu.make_async_remote_copy(
+            src_ref=s2.at[(yy + k) % 4, :, PARTS[h]], dst_ref=r2.at[k - 1, :, PARTS[h]],
+            send_sem=y_ss.at[k - 1, h], recv_sem=y_rs.at[k - 1, h],
+            device_id=ydev(k), device_id_type=MESH,
+        )
+
+    def x3(k, h):
+        return pltpu.make_async_remote_copy(
+            src_ref=s3.at[(xx + k) % 4, :, PARTS[h]], dst_ref=r3.at[k - 1, :, PARTS[h]],
+            send_sem=x_ss.at[k - 1, h], recv_sem=x_rs.at[k - 1, h],
+            device_id=xdev(k), device_id_type=MESH,
+        )
 
     def weights(j, carry):
         gradient(j)
@@ -317,28 +319,32 @@
         @pl.when(j == 2)
         def _():
             combine(0)
-            ring(0).start()
-            ring(1).start()
+            for h in range(2):
+                ring(0, h).start()
+                ring(1, h).start()
 
         @pl.when(j == 3)
         def _():
             combine(1)
-            ring(3).start()
+            ring(3, 0).start()
 
         return carry
 
     lax.fori_loop(0, 4, weights, 0)
 
-    def pass_on():
-        ring(0).wait_recv()
-        onward[0] = (accf[cc, after, low] + ring_in[0].astype(F32)).astype(BF16)
-        ring(4).start()
-        ring(1).wait_recv()
-        onward[1] = (accf[cc, before, high] + ring_in[1].astype(F32)).astype(BF16)
-        ring(5).start()
+    def pass_on(h):
+        cols = PARTS[h]
+        ring(0, h).wait_recv()
+        total = accf[cc, after, low, :, cols] + ring_in[0, :, :, cols].astype(F32)
+        onward[0, :, :, cols] = total.astype(BF16)
+        ring(4, h).start()
+        ring(1, h).wait_recv()
+        total = accf[cc, before, high, :, cols] + ring_in[1, :, :, cols].astype(F32)
+        onward[1, :, :, cols] = total.astype(BF16)
+        ring(5, h).start()
 
     combine(2)
-    ring(2).start()
+    ring(2, 0).start()
 
     def last(m, carry):
         interpolate(m)
@@ -346,7 +352,10 @@
         @pl.when(m == 2)
         def _():
             combine(3)
-            pass_on()
+            pass_on(0)
+            ring(2, 1).start()
+            ring(3, 1).start()
+            pass_on(1)
 
         return carry
 
@@ -363,36 +372,43 @@
         return carry
 
     lax.fori_loop(0, 1, finish, 0)
-    for n in range(2, 6):
-        ring(n).wait_recv()
-    first = accf[cc, z, low] + ring_in[4].astype(F32) + ring_in[3].astype(F32)
-    second = accf[cc, z, high] + ring_in[5].astype(F32) + ring_in[2].astype(F32)
-    p2[0:2] = first
-    p2[2:4] = second
-    s2[0:2] = first.astype(BF16)
-    s2[2:4] = second.astype(BF16)
-    for k in (2, 1, 3):
-        y2(k).start()
-
-    lax.fori_loop(1, 2, finish, 0)
-
-    for k in (1, 3, 2):
-        y2(k).wait_recv()
-    total = p2[yy]
-    for k in range(3):
-        total = total + r2[k].astype(F32)
-    p3[...] = total.reshape(4, 8, CW)
-    for k in (2, 1, 3):
-        x3(k).start()
+    for h in range(2):
+        cols = PARTS[h]
+        for n in range(2, 6):
+            ring(n, h).wait_recv()
+        first = accf[cc, z, low, :, cols] + ring_in[4, :, :, cols].astype(F32)
+        first = first + ring_in[3, :, :, cols].astype(F32)
+        second = accf[cc, z, high, :, cols] + ring_in[5, :, :, cols].astype(F32)
+        second = second + ring_in[2, :, :, cols].astype(F32)
+        p2[0:2, :, cols] = first
+        p2[2:4, :, cols] = second
+        s2[0:2, :, cols] = first.astype(BF16)
+        s2[2:4, :, cols] = second.astype(BF16)
+        for k in (2, 1, 3):
+            y2(k, h).start()
+
+    for h in range(2):
+        cols = PARTS[h]
+        for k in (1, 3, 2):
+            y2(k, h).wait_recv()
+        total = p2[yy, :, cols]
+        for k in range(3):
+            total = total + r2[k, :, cols].astype(F32)
+        total = total.reshape(4, 8, cols.stop - cols.start)
+        p3[:, :, cols] = total
+        s3[:, :, cols] = total.astype(BF16)
+        for k in (2, 1, 3):
+            x3(k, h).start()
     dn_copy(3, 1).start()
     up_copy(3, 1).start()
-    lax.fori_loop(2, 3, finish, 0)
+    lax.fori_loop(1, 3, finish, 0)
 
     for k in (1, 3, 2):
-        x3(k).wait_recv()
+        for h in range(2):
+            x3(k, h).wait_recv()
     total = p3[xx]
     for k in range(3):
-        total = total + r3[k]
+        total = total + r3[k].astype(F32)
     gh_ref[...] = total[:, :1024]
     go_ref[...] = total[:, 1024:]
 
@@ -409,9 +425,11 @@
         c_copy(m).wait_send()
     for k in (1, 2, 3):
         for f in (y2, x3):
-            f(k).wait_send()
+            for h in range(2):
+                f(k, h).wait_send()
     for n in range(6):
-        ring(n).wait_send()
+        for h in range(2):
+            ring(n, h).wait_send()
 
 
 def store(gh_ref, go_ref, mesh_ref, gh_out, go_out, mesh_out, sem):
@@ -445,10 +463,10 @@
         V((2, 4, 4, 32, CW), F32), V((4, 4, 32, CW), BF16), V((4, 4, 32, CW), BF16),
         V((4, 4, 32, CW), BF16), V((6, 2, 32, CW), BF16), V((2, 2, 32, CW), BF16),
         V((4, 32, CW), F32), V((4, 32, CW), BF16), V((3, 32, CW), BF16),
-        V((4, 8, CW), F32), V((3, 8, CW), F32),
+        V((4, 8, CW), F32), V((4, 8, CW), BF16), V((3, 8, CW), BF16),
         D((4,)), D((4,)), D((3,)), D((3,)), D((4, 3)), D((4, 3)),
         D((4, 2)), D((4, 2)), D((4, 2)), D((4, 2)), D((4,)), D((4,)),
-        D((6,)), D((6,)), D((3,)), D((3,)), D((3,)), D((3,)),
+        D((6, 2)), D((6, 2)), D((3, 2)), D((3, 2)), D((3, 2)), D((3, 2)),
     ]
     held = pl.pallas_call(
         kernel,

time: 63.2 us -> 62.6 us (level)
  no operation moved by 1% of the time
where the time goes in v5:
time: 62.6 us; the launch traced here: 62.5 us
  Pallas kernels  61.8 us (99%)
  between operations  0.64 us (1%)
    pallas_call x1, Pallas kernels, body(): pl.pallas_call(kernel, out_shape=(V((8, 1024), F32), V((8, 128), F32), V(...  59.2 us
    pallas_call x1, Pallas kernels, body(): pl.pallas_call(store, out_shape=(jax.ShapeDtypeStruct((8, 1024), F32), ja...  2.66 us

profile of v5, /device:TPU:0, one launch (start us, length us, event | category | flops | bytes accessed | tf_op | source)
XLA Modules:
  0.0 62.5 jit_solution(302347903714838808)
XLA Ops:
  0.6 59.2 %shard_map.112 = (f32[8,1024]{1,0:T(8,128)S(1)}, f32[8,128]{1,0:T(8,128)S(1)}, f32[4,256,1024]{2,1,0:T(8,128)S(1)}) custom-call(bf16[4,512,1024]{2,1,0:T(8,128)(2,1)} %x_hbm.1, bf16[1024,1024]{1,0:T(8,128)(2,1)} %wh_hbm.1, bf16[96,1024]{1,0:T(8,128)(2,1)} %bitcast.4, f32[1,1024]{1,0:T(1,128)} %bitcast.5, f32[1,96]{1,0:T(1,128)} %bitcast.6, f32[1,96]{1,0:T(1,128)} %bitcast.7, ...), custom_call_target="tpu_custom_call" | custom-call | tf_op jit(solution)/shard_map/pallas_call | solution.py:471
  59.8 2.7 %shard_map.113 = (f32[8,1024]{1,0:T(8,128)}, f32[8,96]{1,0:T(8,128)}, f32[4,256,1024]{2,1,0:T(8,128)}) custom-call(f32[8,1024]{1,0:T(8,128)S(1)} %get-tuple-element.6.gh_ref, f32[8,128]{1,0:T(8,128)S(1)} %get-tuple-element.7.go_ref, f32[4,256,1024]{2,1,0:T(8,128)S(1)} %get-tuple-element.8.mesh_ref), custom_call_target="tpu_custom_call" | custom-call | tf_op jit(solution)/shard_map/pallas_call | solution.py:486
